TPU v7x, 32 devices: a whole 2x2x4 slice. The times are simulated.
32 devices in a mesh: grp: 4 (over z), gx: 4 (over y, x), gy: 2 (over core).
Axes of the slice: x: 2, y: 2, z: 4, core: 2. Of those that a mesh axis runs over, the one named last changes fastest.
Arguments:
- fluid_temp: float32 [64, 256, 1024], P('gx', 'gy', 'grp'), may hold values from -6 to 6
- active: int32 [64, 256, 1024], P('gx', 'gy', 'grp'), may hold values 0 or 1
- fin_temp: float32 [256, 128, 512], P('grp', 'gx', 'gy'), may hold values from -6 to 6
- fin_source: float32 [256, 128, 512], P('grp', 'gx', 'gy'), may hold values from -6 to 6
- wall_owner: int32 [4, 2, 2048, 1], P('gx', 'gy'), may hold values from 0 to 3, as said below
- wall_target: int32 [4, 2, 2048], P('gx', 'gy'), may hold values from 0 to 8191, as said below
Outputs:
- fluid_new: float32 [64, 256, 1024], P('gx', 'gy', 'grp')
- fin_new: float32 [256, 128, 512], P('grp', 'gx', 'gy')
Inputs may be any that keep to these rules, and one draw needn't show every extreme that they name: `wall_owner`: among the 2048 wall cells of one column block (a, b), exactly 1024 name the owner a and at most 1024 name any one owner; in every draw one owner is named by exactly 1024 wall cells of every column block. `wall_target`: wall cell w = i * 128 + j names a root cell (2 * i + di) * 256 + 2 * j + dj of the 2 x 2 patch beneath it, di and dj being 0 or 1; the first wall cell of a block names its patch's first root cell, the last one its patch's last.
All inputs are finite; a program needn't handle non-finite values. No bound on the sum of `active` on one device may be relied on, other than what follows from the above.
Results may differ from a plain program's by a relative error of at most 0.00002.
Values sent between devices are 32-bit elements; how exact they have to be, the bound alone decides.
No kernel may reach another device: no remote copies, remote signals or barrier semaphores. Data moves between devices by JAX's collectives and lax.ppermute only.
A program may use at most 64 MiB of HBM per device.

v0:
```python
import jax
import jax.numpy as jnp
from jax import lax
from jax.sharding import PartitionSpec as P

FLUID_DIFFUSION = 1.0
FIN_CONDUCTION = 1.0
HEAT_COEF = 1.0


def padded_2(block, sides, width):
    for axis, dim in sides:
        count = lax.axis_size(axis)
        forward = [(i, i + 1) for i in range(count - 1)]
        backward = [(target, source) for source, target in forward]
        low = lax.ppermute(
            lax.slice_in_dim(block, block.shape[dim] - width, None, axis=dim), axis, forward
        )
        high = lax.ppermute(lax.slice_in_dim(block, 0, width, axis=dim), axis, backward)
        block = jnp.concatenate([low, block, high], axis=dim)
    return block


def six_sum(padded):
    return (
        padded[2:, 1:-1, 1:-1]
        + padded[:-2, 1:-1, 1:-1]
        + padded[1:-1, 2:, 1:-1]
        + padded[1:-1, :-2, 1:-1]
        + padded[1:-1, 1:-1, 2:]
        + padded[1:-1, 1:-1, :-2]
    )


def fluid_padded_deep(field):
    return padded_2(field, (("grp", 2), ("gx", 0), ("gy", 1)), 1)


def fin_first_wide(start_state, fin_rhs):
    extended = padded_2(jnp.stack([start_state, fin_rhs]), (("grp", 1), ("gx", 2), ("gy", 3)), 2)
    state_ext = extended[0]
    rhs_ext = extended[1]
    inner = state_ext[1:-1, 1:-1, 1:-1]
    diag = 1.0 + 6.0 * FIN_CONDUCTION
    image = diag * inner - FIN_CONDUCTION * six_sum(state_ext)
    first_wide = inner + (rhs_ext[1:-1, 1:-1, 1:-1] - image) / diag
    fin_depth, fin_width, fin_height = start_state.shape
    shape = first_wide.shape
    depth_pos = lax.axis_index("grp") * fin_depth - 1 + lax.broadcasted_iota(jnp.int32, shape, 0)
    width_pos = lax.axis_index("gx") * fin_width - 1 + lax.broadcasted_iota(jnp.int32, shape, 1)
    height_pos = lax.axis_index("gy") * fin_height - 1 + lax.broadcasted_iota(jnp.int32, shape, 2)
    inside = (
        (depth_pos >= 0)
        & (depth_pos < fin_depth * lax.axis_size("grp"))
        & (width_pos >= 0)
        & (width_pos < fin_width * lax.axis_size("gx"))
        & (height_pos >= 0)
        & (height_pos < fin_height * lax.axis_size("gy"))
    )
    return jnp.where(inside, first_wide, 0.0)


def fluid_update(padded, field, fluid_temp, update_mask, ghost, on_wall):
    lowest = lax.broadcasted_iota(jnp.int32, field.shape, 2) == 0
    below = jnp.where(lowest & on_wall, ghost[:, :, None], 0.0)
    neighbours = six_sum(padded) + below
    updated = (fluid_temp + FLUID_DIFFUSION * neighbours) / (1.0 + 6.0 * FLUID_DIFFUSION)
    return jnp.where(update_mask, updated, field)


def local(fluid_temp, active, fin_temp, fin_source, wall_owner, wall_target):
    first_cells, second_cells, third_cells = fluid_temp.shape
    fin_depth, fin_width, fin_height = fin_temp.shape
    owner_count = lax.axis_size("gx")
    wall_cells = first_cells * second_cells
    capacity = min(wall_cells, max(2, 2 * wall_cells // owner_count))
    on_wall = lax.axis_index("grp") == 0
    owners = wall_owner[0, 0, :, 0]
    targets = wall_target[0, 0, :]
    onehot = (owners[:, None] == jnp.arange(owner_count, dtype=jnp.int32)[None, :]).astype(
        jnp.int32
    )
    ranks = jnp.sum((jnp.cumsum(onehot, axis=0) - onehot) * onehot, axis=1)
    slot_index = owners * capacity + ranks
    wall_temps = fluid_temp[:, :, 0].reshape(-1)
    send_temps = jnp.zeros((owner_count * capacity,), jnp.float32).at[slot_index].set(wall_temps)
    send_targets = (
        jnp.full((owner_count * capacity,), -1.0, jnp.float32)
        .at[slot_index]
        .set(targets.astype(jnp.float32))
    )
    received = lax.all_to_all(
        jnp.stack([send_temps, send_targets]), "gx", split_axis=1, concat_axis=1, tiled=True
    )
    got_targets = received[1].astype(jnp.int32)
    valid = (got_targets >= 0) & on_wall
    safe_targets = jnp.where(valid, got_targets, 0)
    surface = fin_temp[0].reshape(-1)
    fin_wall = jnp.where(valid, surface[safe_targets], 0.0)
    heat_flux = jnp.where(valid, HEAT_COEF * (received[0] - fin_wall), 0.0)
    deposit = jax.ops.segment_sum(heat_flux, safe_targets, num_segments=fin_width * fin_height)
    returned = lax.all_to_all(fin_wall, "gx", split_axis=0, concat_axis=0, tiled=True)
    ghost = returned[slot_index].reshape(first_cells, second_cells)
    fin_rhs = fin_temp + fin_source
    fin_rhs = fin_rhs.at[0].add(deposit.reshape(fin_width, fin_height))
    diag = 1.0 + 6.0 * FIN_CONDUCTION
    spectral = 6.0 * FIN_CONDUCTION / diag
    omega = 1.0 / (1.0 - spectral * spectral / 2.0)
    shape = fluid_temp.shape
    colour = (
        lax.broadcasted_iota(jnp.int32, shape, 0)
        + lax.broadcasted_iota(jnp.int32, shape, 1)
        + lax.broadcasted_iota(jnp.int32, shape, 2)
    ) % 2
    red_mask = (colour == 0) & (active == 1)
    black_mask = (colour == 1) & (active == 1)
    first_wide = fin_first_wide(fin_temp, fin_rhs)
    first_state = first_wide[1:-1, 1:-1, 1:-1]
    second_image = diag * first_state - FIN_CONDUCTION * six_sum(first_wide)
    red_temp = fluid_update(
        fluid_padded_deep(fluid_temp), fluid_temp, fluid_temp, red_mask, ghost, on_wall
    )
    fluid_new = fluid_update(
        fluid_padded_deep(red_temp), red_temp, fluid_temp, black_mask, ghost, on_wall
    )
    fin_new = omega * (first_state + (fin_rhs - second_image) / diag - fin_temp) + fin_temp
    return (fluid_new, fin_new)


def solution(mesh):
    in_specs = (
        P("gx", "gy", "grp"),
        P("gx", "gy", "grp"),
        P("grp", "gx", "gy"),
        P("grp", "gx", "gy"),
        P("gx", "gy", None, None),
        P("gx", "gy", None),
    )
    out_specs = (P("gx", "gy", "grp"), P("grp", "gx", "gy"))
    return jax.shard_map(local, mesh=mesh, in_specs=in_specs, out_specs=out_specs, check_vma=False)
```

profile of v0, /device:TPU:12, one launch (start us, length us, event | category | flops | bytes accessed | tf_op | source)
XLA Modules:
  0.0 259.6 jit_solution(15178382803053533291)
XLA Ops:
  0.6 2.9 %fusion.49 = (f32[16,128,1]{2,1,0:T(8,128)}, f32[16,128,1]{2,1,0:T(8,128)S(1)}) fusion(f32[16,128,256]{2,1,0:T(8,128)} %param.8), kind=kLoop, calls=%fused_computation.146 | loop fusion | bytes 32768 | tf_op jit(solution)/shard_map/slice | solution.py:19
  5.2 2.4 collective-permute-start.1
  9.3 8.1 %scatter_custom_fusion = f32[4096]{0:T(1024)S(1)} fusion(s32[2048]{0:T(1024)S(1)} %bitcast.88, f32[2048]{0:T(1024)S(1)} %bitcast.94, f32[]{:T(128)} %constant.86.clone.1), kind=kCustom, calls=%fused_computation.130 | custom fusion | bytes 16388 | tf_op jit(solution)/shard_map/scatter | solution.py:86
  17.4 8.1 %scatter_custom_fusion.1 = f32[4096]{0:T(1024)S(1)} fusion(s32[2048]{0:T(1024)S(1)} %bitcast.89, f32[2048]{0:T(1024)S(1)} %bitcast.96, f32[]{:T(128)} %constant.89.clone.1), kind=kCustom, calls=%fused_computation.128 | custom fusion | bytes 16388 | tf_op jit(solution)/shard_map/scatter | solution.py:90
  26.1 4.2 %all-to-all-start = ((f32[2,4,1024]{2,0,1:T(2,128)}), f32[2,4,1024]{2,0,1:T(2,128)S(1)}, u32[]{:S(2)}, u32[]{:S(2)}) async-start(f32[2,4,1024]{2,0,1:T(2,128)} %pad_maximum_fusion.52), calls=%async_computation | async-start | bytes 65536 | tf_op jit(solution)/shard_map/all_to_all | solution.py:92
  30.7 3.5 %collective-permute-start = (f32[16,128,1]{1,0,2:T(8,128)S(1)}, f32[16,128,1]{1,0,2:T(8,128)S(1)}, u32[]{:S(2)}, u32[]{:S(2)}) collective-permute-start(f32[16,128,1]{1,0,2:T(8,128)S(1)} %copy.78), channel_id=1, source_target_pairs={{0,8},{8,16},{16,24},{1,9},{9,17},{17,25},{2,10},{10,18},{18,26},{... | collective-permute-start | bytes 24584 | tf_op jit(solution)/shard_map/ppermute | solution.py:16
  35.6 1.8 copy.70
  37.4 2.8 %add.197 = f32[64,32,256]{2,1,0:T(8,128)S(1)} add(f32[64,32,256]{2,1,0:T(8,128)} %param.10, f32[64,32,256]{2,1,0:T(8,128)} %param.11) | non-fusion elementwise | flops 524288 | bytes 6291456 | tf_op jit(solution)/shard_map/add | solution.py:104
  40.2 2.9 %copy.43 = s32[16,128,256]{1,2,0:T(8,128)} copy(s32[16,128,256]{2,1,0:T(8,128)} %param.9) | data formatting | bytes 4194304 | tf_op args[1]
  44.1 3.4 %collective-permute-start.2 = (f32[1,128,258]{1,2,0:T(8,128)S(1)}, f32[1,128,258]{1,2,0:T(8,128)S(1)}, u32[]{:S(2)}, u32[]{:S(2)}) collective-permute-start(f32[1,128,258]{1,2,0:T(8,128)S(1)} %get-tuple-element.41), channel_id=1, source_target_pairs={{2,0},{4,2},{6,4},{3,1},{5,3},{7,5},{10,8},{12,10},{14,12},{11,9},... | collective-permute-start | bytes 396296 | tf_op jit(solution)/shard_map/ppermute | solution.py:19
  47.4 2.5 collective-permute-start.3
  50.0 23.0 %gather_fusion = f32[4096]{0:T(1024)S(1)} fusion(f32[8192]{0:T(1024)S(1)} %bitcast.57, s32[4096]{0:T(1024)S(1)} %broadcast_clamp_fusion), kind=kCustom, calls=%fused_computation | custom fusion | bytes 49152 | tf_op jit(solution)/shard_map/gather | solution.py:99
  73.2 28.8 %scatter_custom_fusion.2 = f32[8192]{0:T(1024)S(1)} fusion(s32[4096]{0:T(1024)S(1)} %bitcast.92, f32[4096]{0:T(1024)S(1)} %subtract_select_fusion, f32[]{:T(128)} %constant.86.clone.1), kind=kCustom, calls=%fused_computation.123 | custom fusion | flops 4096 | bytes 32772 | tf_op jit(solution)/shard_map/scatter-add | solution.py:101
  102.7 4.2 %all-to-all-start.1 = ((f32[4,1024,1]{1,2,0:T(1,128)}), f32[4,1024,1]{1,2,0:T(1,128)S(1)}, u32[]{:S(2)}, u32[]{:S(2)}) async-start(f32[4,1024,1]{1,2,0:T(1,128)} %copy.57), calls=%async_computation.1 | async-start | bytes 32768 | tf_op jit(solution)/shard_map/all_to_all | solution.py:102
  108.6 2.9 %fusion.47 = (f32[18,1,258]{1,2,0:T(8,128)}, f32[18,1,258]{1,2,0:T(8,128)}) fusion(f32[18,128,258]{1,2,0:T(8,128)S(1)} %pad_maximum_fusion.2), kind=kLoop, calls=%fused_computation.144 | loop fusion | bytes 74304 | tf_op jit(solution)/shard_map/slice | solution.py:19
  111.6 3.0 %copy.49 = f32[18,1,258]{2,0,1:T(8,128)S(1)} copy(f32[18,1,258]{1,2,0:T(8,128)} %get-tuple-element.36) | data formatting | bytes 37152 | tf_op jit(solution)/shard_map/slice | solution.py:19
  115.9 3.0 %copy.51 = f32[18,1,258]{2,0,1:T(8,128)S(1)} copy(f32[18,1,258]{1,2,0:T(8,128)} %get-tuple-element.37) | data formatting | bytes 37152 | tf_op jit(solution)/shard_map/slice | solution.py:17
  119.0 3.2 %collective-permute-start.5 = (f32[18,1,258]{2,0,1:T(8,128)S(1)}, f32[18,1,258]{2,0,1:T(8,128)S(1)}, u32[]{:S(2)}, u32[]{:S(2)}) collective-permute-start(f32[18,1,258]{2,0,1:T(8,128)S(1)} %copy.51), channel_id=1, source_target_pairs={{0,1},{2,3},{4,5},{6,7},{8,9},{10,11},{12,13},{14,15},{16,17},{18,... | collective-permute-start | bytes 55736 | tf_op jit(solution)/shard_map/ppermute | solution.py:16
  122.2 11.8 %gather_fusion.1 = f32[2048]{0:T(1024)S(1)} fusion(f32[4096]{0:T(1024)S(1)} %bitcast.58, s32[2048]{0:T(1024)S(1)} %broadcast_clamp_fusion.1), kind=kCustom, calls=%fused_computation.1 | custom fusion | bytes 24576 | tf_op jit(solution)/shard_map/gather | solution.py:103
  134.0 2.2 copy.50
  136.2 2.2 copy.52
  138.5 11.2 %fusion.7 = (f32[16,128,256]{1,2,0:T(8,128)S(1)}, pred[16,128,256]{1,2,0:T(8,128)(4,1)S(1)}) fusion(f32[16,128,256]{1,2,0:T(8,128)} %copy.70, f32[16,128,1]{1,2,0:T(1,128)S(1)} %bitcast.72, f32[16,128,1]{1,2,0:T(1,128)S(1)} %bitcast.69, f32[18,1,258]{1,2,0:T(8,128)} %copy.52, f32[1,128,258]{1,2,0:T(8,128)S(1)} %collective-permute-done.2, ...), kind=kLoop, calls=%fused_computation.28 | loop fusion | flops 23068672 | bytes 7141920 | tf_op jit(solution)/shard_map/jit(_where)/select_n | solution.py:68
  149.7 3.5 %collective-permute-start.6 = (f32[16,128,1]{1,0,2:T(8,128)S(1)}, f32[16,128,1]{1,0,2:T(8,128)S(1)}, u32[]{:S(2)}, u32[]{:S(2)}) collective-permute-start(f32[16,128,1]{1,0,2:T(8,128)S(1)} %bitcast.98), channel_id=1, source_target_pairs={{0,8},{8,16},{16,24},{1,9},{9,17},{17,25},{2,10},{10,18},{18,26},{... | collective-permute-start | bytes 24584 | tf_op jit(solution)/shard_map/ppermute | solution.py:16
  153.2 2.4 collective-permute-start.7
  155.6 3.5 %collective-permute-start.12 = (f32[2,2,32,256]{3,2,1,0:T(8,128)S(1)}, f32[2,2,32,256]{3,2,1,0:T(8,128)S(1)}, u32[]{:S(2)}, u32[]{:S(2)}) collective-permute-start(f32[2,2,32,256]{3,2,1,0:T(8,128)S(1)} %get-tuple-element.32), channel_id=1, source_target_pairs={{0,8},{8,16},{16,24},{1,9},{9,17},{17,25},{2,10},{10,18},{18,26},{... | collective-permute-start | bytes 393224 | tf_op jit(solution)/shard_map/ppermute | solution.py:16
  159.1 2.4 collective-permute-start.13
  162.2 3.4 %collective-permute-start.8 = (f32[1,128,258]{1,2,0:T(8,128)}, f32[1,128,258]{1,2,0:T(8,128)}, u32[]{:S(2)}, u32[]{:S(2)}) collective-permute-start(f32[1,128,258]{1,2,0:T(8,128)} %get-tuple-element.39), channel_id=1, source_target_pairs={{2,0},{4,2},{6,4},{3,1},{5,3},{7,5},{10,8},{12,10},{14,12},{11,9},... | collective-permute-start | bytes 396296 | tf_op jit(solution)/shard_map/ppermute | solution.py:19
  165.6 3.1 %collective-permute-start.9 = (f32[1,128,258]{1,2,0:T(8,128)}, f32[1,128,258]{1,2,0:T(8,128)}, u32[]{:S(2)}, u32[]{:S(2)}) collective-permute-start(f32[1,128,258]{1,2,0:T(8,128)} %get-tuple-element.38), channel_id=1, source_target_pairs={{0,2},{2,4},{4,6},{1,3},{3,5},{5,7},{8,10},{10,12},{12,14},{9,11},... | collective-permute-start | bytes 396296 | tf_op jit(solution)/shard_map/ppermute | solution.py:16
  169.3 2.4 pad_maximum_fusion.43
  171.6 1.9 collective-permute-start.14
  173.5 4.8 %collective-permute-start.15 = (f32[2,68,2,256]{3,2,1,0:T(2,128)}, f32[2,68,2,256]{3,2,1,0:T(2,128)S(1)}, u32[]{:S(2)}, u32[]{:S(2)}) collective-permute-start(f32[2,68,2,256]{3,2,1,0:T(2,128)} %get-tuple-element.31), channel_id=1, source_target_pairs={{2,0},{4,2},{6,4},{3,1},{5,3},{7,5},{10,8},{12,10},{14,12},{11,9},... | collective-permute-start | bytes 835592 | tf_op jit(solution)/shard_map/ppermute | solution.py:19
  179.6 2.9 %fusion.46 = (f32[18,1,258]{1,2,0:T(8,128)}, f32[18,1,258]{1,2,0:T(8,128)}) fusion(f32[18,128,258]{1,2,0:T(8,128)S(1)} %pad_maximum_fusion.3), kind=kLoop, calls=%fused_computation.143 | loop fusion | bytes 74304 | tf_op jit(solution)/shard_map/slice | solution.py:19
  182.5 3.0 %copy.64 = f32[18,1,258]{2,0,1:T(8,128)S(1)} copy(f32[18,1,258]{1,2,0:T(8,128)} %get-tuple-element.34) | data formatting | bytes 37152 | tf_op jit(solution)/shard_map/slice | solution.py:19
  186.8 3.7 %copy.66 = f32[18,1,258]{2,0,1:T(8,128)} copy(f32[18,1,258]{1,2,0:T(8,128)} %get-tuple-element.35) | data formatting | bytes 37152 | tf_op jit(solution)/shard_map/slice | solution.py:17
  190.5 3.6 %collective-permute-start.11 = (f32[18,1,258]{2,0,1:T(8,128)}, f32[18,1,258]{2,0,1:T(8,128)}, u32[]{:S(2)}, u32[]{:S(2)}) collective-permute-start(f32[18,1,258]{2,0,1:T(8,128)} %copy.66), channel_id=1, source_target_pairs={{0,1},{2,3},{4,5},{6,7},{8,9},{10,11},{12,13},{14,15},{16,17},{18,... | collective-permute-start | bytes 55736 | tf_op jit(solution)/shard_map/ppermute | solution.py:16
  194.6 2.3 copy.65
  196.9 3.0 %copy.67 = f32[18,1,258]{1,2,0:T(8,128)} copy(f32[18,1,258]{2,0,1:T(8,128)} %collective-permute-done.11) | data formatting | bytes 37152 | tf_op jit(solution)/shard_map/ppermute | solution.py:16
  200.0 2.5 pad_maximum_fusion.1
  202.4 3.3 %fusion.45 = (f32[2,68,36,2]{3,2,1,0:T(8,128)}, f32[2,68,36,2]{3,2,1,0:T(8,128)}) fusion(f32[2,68,36,256]{3,2,1,0:T(8,128)S(1)} %pad_maximum_fusion.1), kind=kLoop, calls=%fused_computation.142 | loop fusion | bytes 156672 | tf_op jit(solution)/shard_map/slice | solution.py:17
  205.8 2.7 %copy.71 = f32[2,68,36,2]{1,3,2,0:T(2,128)S(1)} copy(f32[2,68,36,2]{3,2,1,0:T(8,128)} %get-tuple-element.28) | data formatting | bytes 78336 | tf_op jit(solution)/shard_map/slice | solution.py:17
  209.9 2.7 %copy.72 = f32[2,68,36,2]{1,3,2,0:T(2,128)S(1)} copy(f32[2,68,36,2]{3,2,1,0:T(8,128)} %get-tuple-element.29) | data formatting | bytes 78336 | tf_op jit(solution)/shard_map/slice | solution.py:19
  214.1 12.0 %fusion.10 = f32[16,128,256]{1,2,0:T(8,128)} fusion(f32[16,128,256]{1,2,0:T(8,128)} %copy-done.2, f32[16,128,256]{1,2,0:T(8,128)} %copy.70, f32[16,128,1]{1,2,0:T(1,128)S(1)} %bitcast.75, f32[16,128,1]{1,2,0:T(1,128)S(1)} %bitcast.78, f32[18,1,258]{1,2,0:T(8,128)} %copy.67, f32[1,128,258]{1,2,0:T(8,128)} %collective-permute-done.8, ...), kind=kLoop, calls=%fused_computation.31 | loop fusion | flops 22544384 | bytes 7141920 | tf_op jit(solution)/shard_map/jit(_where)/select_n | solution.py:68
  226.1 2.9 %copy.75 = f32[16,128,256]{2,1,0:T(8,128)} copy(f32[16,128,256]{1,2,0:T(8,128)} %fusion.10) | data formatting | bytes 4194304
  229.0 2.6 %copy.73 = f32[2,68,36,2]{3,2,1,0:T(8,128)} copy(f32[2,68,36,2]{1,3,2,0:T(2,128)S(1)} %collective-permute-done.16) | data formatting | bytes 78336 | tf_op jit(solution)/shard_map/ppermute | solution.py:16
  231.6 2.6 copy.74
  234.2 11.1 %pad_maximum_fusion = f32[2,68,36,260]{3,2,1,0:T(8,128)S(1)} fusion(f32[2,68,36,2]{3,2,1,0:T(8,128)} %copy.74, f32[2,68,2,256]{3,2,1,0:T(2,128)} %copy-done.5, f32[2,2,32,256]{3,2,1,0:T(8,128)S(1)} %collective-permute-done.13, f32[1,64,32,256]{3,2,1,0:T(8,128)S(1)} %bitcast.62, f32[1,64,32,256]{3,2,1,0:T(8,128)} %bitcast.65, ...), kind=kLoop, calls=%fused_computation.5 | loop fusion | flops 8910720 | bytes 10183680 | tf_op jit(solution)/shard_map/concatenate | solution.py:20
  246.0 8.7 %fusion.4 = f32[66,34,258]{2,1,0:T(8,128)S(1)} fusion(f32[68,36,260]{2,1,0:T(8,128)S(1)} %get-tuple-element.27, f32[68,36,260]{2,1,0:T(8,128)S(1)} %get-tuple-element.26, pred[34]{0:T(512)(128)(4,1)S(1)} %copy-done.10, pred[258]{0:T(512)(128)(4,1)S(1)} %copy-done.12, pred[258]{0:T(512)(128)(4,1)S(1)} %copy-done.13, pred[34]{0:T(512)(128)(4,1)S(1)} %copy-done.11, ...), kind=kLoop, calls=%fused_computation.14 | loop fusion | flops 8684280 | bytes 20842922 | tf_op jit(solution)/shard_map/jit(_where)/select_n | solution.py:60
  254.7 4.9 %fusion.18 = f32[64,32,256]{2,1,0:T(8,128)} fusion(f32[64,32,256]{2,1,0:T(8,128)S(1)} %copy-done.1, f32[64,32,256]{2,1,0:T(8,128)S(1)} %fusion.32, f32[66,34,258]{2,1,0:T(8,128)S(1)} %fusion.4), kind=kLoop, calls=%fused_computation.40 | loop fusion | flops 6815744 | bytes 20971520 | tf_op jit(solution)/shard_map/add | solution.py:126
  (89 shorter events, 18.5 us)
Async XLA Ops:
  0.6 7.0 %copy-start.6 = (s32[1,1,2048,1]{2,3,1,0:T(1,128)S(1)}, s32[1,1,2048,1]{2,3,1,0:T(1,128)}, u32[]{:S(2)}) copy-start(s32[1,1,2048,1]{2,3,1,0:T(1,128)} %param.12) | copy-start | bytes 24580
  0.6 8.7 %copy-start.7 = (s32[1,1,2048]{2,1,0:T(1,128)S(1)}, s32[1,1,2048]{2,1,0:T(1,128)}, u32[]{:S(2)}) copy-start(s32[1,1,2048]{2,1,0:T(1,128)} %param.13) | copy-start | bytes 24580
  3.5 32.0 %copy-start.4 = (f32[16,128,256]{2,1,0:T(8,128)S(1)}, f32[16,128,256]{2,1,0:T(8,128)}, u32[]{:S(2)}) copy-start(f32[16,128,256]{2,1,0:T(8,128)} %param.8) | copy-start | bytes 6291460
  5.2 37.8 %collective-permute-start.1 = (f32[16,128,1]{1,0,2:T(8,128)S(1)}, f32[16,128,1]{1,0,2:T(8,128)S(1)}, u32[]{:S(2)}, u32[]{:S(2)}) collective-permute-start(f32[16,128,1]{1,0,2:T(8,128)S(1)} %copy.77), channel_id=1, source_target_pairs={{8,0},{16,8},{24,16},{9,1},{17,9},{25,17},{10,2},{18,10},{26,18},{... | collective-permute-start | bytes 24584 | tf_op jit(solution)/shard_map/ppermute | solution.py:19
  26.1 23.8 %all-to-all-start = ((f32[2,4,1024]{2,0,1:T(2,128)}), f32[2,4,1024]{2,0,1:T(2,128)S(1)}, u32[]{:S(2)}, u32[]{:S(2)}) async-start(f32[2,4,1024]{2,0,1:T(2,128)} %pad_maximum_fusion.52), calls=%async_computation | async-start | bytes 65536 | tf_op jit(solution)/shard_map/all_to_all | solution.py:92
  30.7 12.4 %collective-permute-start = (f32[16,128,1]{1,0,2:T(8,128)S(1)}, f32[16,128,1]{1,0,2:T(8,128)S(1)}, u32[]{:S(2)}, u32[]{:S(2)}) collective-permute-start(f32[16,128,1]{1,0,2:T(8,128)S(1)} %copy.78), channel_id=1, source_target_pairs={{0,8},{8,16},{16,24},{1,9},{9,17},{17,25},{2,10},{10,18},{18,26},{... | collective-permute-start | bytes 24584 | tf_op jit(solution)/shard_map/ppermute | solution.py:16
  35.5 102.9 %copy-start.8 = (pred[256]{0:T(512)(128)(4,1)}, pred[256]{0:T(512)(128)(4,1)S(1)}, u32[]{:S(2)}) copy-start(pred[256]{0:T(512)(128)(4,1)S(1)} %compare_and_fusion.2) | copy-start | bytes 772
  44.1 62.8 %collective-permute-start.2 = (f32[1,128,258]{1,2,0:T(8,128)S(1)}, f32[1,128,258]{1,2,0:T(8,128)S(1)}, u32[]{:S(2)}, u32[]{:S(2)}) collective-permute-start(f32[1,128,258]{1,2,0:T(8,128)S(1)} %get-tuple-element.41), channel_id=1, source_target_pairs={{2,0},{4,2},{6,4},{3,1},{5,3},{7,5},{10,8},{12,10},{14,12},{11,9},... | collective-permute-start | bytes 396296 | tf_op jit(solution)/shard_map/ppermute | solution.py:19
  47.4 59.4 %collective-permute-start.3 = (f32[1,128,258]{1,2,0:T(8,128)S(1)}, f32[1,128,258]{1,2,0:T(8,128)S(1)}, u32[]{:S(2)}, u32[]{:S(2)}) collective-permute-start(f32[1,128,258]{1,2,0:T(8,128)S(1)} %get-tuple-element.40), channel_id=1, source_target_pairs={{0,2},{2,4},{4,6},{1,3},{3,5},{5,7},{8,10},{10,12},{12,14},{9,11},... | collective-permute-start | bytes 396296 | tf_op jit(solution)/shard_map/ppermute | solution.py:16
  102.7 19.5 %all-to-all-start.1 = ((f32[4,1024,1]{1,2,0:T(1,128)}), f32[4,1024,1]{1,2,0:T(1,128)S(1)}, u32[]{:S(2)}, u32[]{:S(2)}) async-start(f32[4,1024,1]{1,2,0:T(1,128)} %copy.57), calls=%async_computation.1 | async-start | bytes 32768 | tf_op jit(solution)/shard_map/all_to_all | solution.py:102
  114.6 19.4 %collective-permute-start.4 = (f32[18,1,258]{2,0,1:T(8,128)S(1)}, f32[18,1,258]{2,0,1:T(8,128)S(1)}, u32[]{:S(2)}, u32[]{:S(2)}) collective-permute-start(f32[18,1,258]{2,0,1:T(8,128)S(1)} %copy.49), channel_id=1, source_target_pairs={{1,0},{3,2},{5,4},{7,6},{9,8},{11,10},{13,12},{15,14},{17,16},{19,... | collective-permute-start | bytes 55736 | tf_op jit(solution)/shard_map/ppermute | solution.py:19
  119.0 17.3 %collective-permute-start.5 = (f32[18,1,258]{2,0,1:T(8,128)S(1)}, f32[18,1,258]{2,0,1:T(8,128)S(1)}, u32[]{:S(2)}, u32[]{:S(2)}) collective-permute-start(f32[18,1,258]{2,0,1:T(8,128)S(1)} %copy.51), channel_id=1, source_target_pairs={{0,1},{2,3},{4,5},{6,7},{8,9},{10,11},{12,13},{14,15},{16,17},{18,... | collective-permute-start | bytes 55736 | tf_op jit(solution)/shard_map/ppermute | solution.py:16
  138.5 17.1 %copy-start = (f32[64,32,256]{2,1,0:T(8,128)S(1)}, f32[64,32,256]{2,1,0:T(8,128)}, u32[]{:S(2)}) copy-start(f32[64,32,256]{2,1,0:T(8,128)} %param.10) | copy-start | bytes 6291460
  149.7 11.8 %copy-start.2 = (f32[16,128,256]{1,2,0:T(8,128)}, f32[16,128,256]{1,2,0:T(8,128)S(1)}, u32[]{:S(2)}) copy-start(f32[16,128,256]{1,2,0:T(8,128)S(1)} %get-tuple-element.22) | copy-start | bytes 6291460
  149.7 11.8 %collective-permute-start.6 = (f32[16,128,1]{1,0,2:T(8,128)S(1)}, f32[16,128,1]{1,0,2:T(8,128)S(1)}, u32[]{:S(2)}, u32[]{:S(2)}) collective-permute-start(f32[16,128,1]{1,0,2:T(8,128)S(1)} %bitcast.98), channel_id=1, source_target_pairs={{0,8},{8,16},{16,24},{1,9},{9,17},{17,25},{2,10},{10,18},{18,26},{... | collective-permute-start | bytes 24584 | tf_op jit(solution)/shard_map/ppermute | solution.py:16
  153.2 8.3 %collective-permute-start.7 = (f32[16,128,1]{1,0,2:T(8,128)S(1)}, f32[16,128,1]{1,0,2:T(8,128)S(1)}, u32[]{:S(2)}, u32[]{:S(2)}) collective-permute-start(f32[16,128,1]{1,0,2:T(8,128)S(1)} %bitcast.97), channel_id=1, source_target_pairs={{8,0},{16,8},{24,16},{9,1},{17,9},{25,17},{10,2},{18,10},{26,18},{... | collective-permute-start | bytes 24584 | tf_op jit(solution)/shard_map/ppermute | solution.py:19
  155.6 13.6 %collective-permute-start.12 = (f32[2,2,32,256]{3,2,1,0:T(8,128)S(1)}, f32[2,2,32,256]{3,2,1,0:T(8,128)S(1)}, u32[]{:S(2)}, u32[]{:S(2)}) collective-permute-start(f32[2,2,32,256]{3,2,1,0:T(8,128)S(1)} %get-tuple-element.32), channel_id=1, source_target_pairs={{0,8},{8,16},{16,24},{1,9},{9,17},{17,25},{2,10},{10,18},{18,26},{... | collective-permute-start | bytes 393224 | tf_op jit(solution)/shard_map/ppermute | solution.py:16
  159.1 10.2 %collective-permute-start.13 = (f32[2,2,32,256]{3,2,1,0:T(8,128)S(1)}, f32[2,2,32,256]{3,2,1,0:T(8,128)S(1)}, u32[]{:S(2)}, u32[]{:S(2)}) collective-permute-start(f32[2,2,32,256]{3,2,1,0:T(8,128)S(1)} %get-tuple-element.33), channel_id=1, source_target_pairs={{8,0},{16,8},{24,16},{9,1},{17,9},{25,17},{10,2},{18,10},{26,18},{... | collective-permute-start | bytes 393224 | tf_op jit(solution)/shard_map/ppermute | solution.py:19
  162.2 16.1 %collective-permute-start.8 = (f32[1,128,258]{1,2,0:T(8,128)}, f32[1,128,258]{1,2,0:T(8,128)}, u32[]{:S(2)}, u32[]{:S(2)}) collective-permute-start(f32[1,128,258]{1,2,0:T(8,128)} %get-tuple-element.39), channel_id=1, source_target_pairs={{2,0},{4,2},{6,4},{3,1},{5,3},{7,5},{10,8},{12,10},{14,12},{11,9},... | collective-permute-start | bytes 396296 | tf_op jit(solution)/shard_map/ppermute | solution.py:19
  165.6 12.8 %collective-permute-start.9 = (f32[1,128,258]{1,2,0:T(8,128)}, f32[1,128,258]{1,2,0:T(8,128)}, u32[]{:S(2)}, u32[]{:S(2)}) collective-permute-start(f32[1,128,258]{1,2,0:T(8,128)} %get-tuple-element.38), channel_id=1, source_target_pairs={{0,2},{2,4},{4,6},{1,3},{3,5},{5,7},{8,10},{10,12},{12,14},{9,11},... | collective-permute-start | bytes 396296 | tf_op jit(solution)/shard_map/ppermute | solution.py:16
  169.3 9.1 %copy-start.3 = (f32[16,128,256]{1,2,0:T(8,128)S(1)}, f32[16,128,256]{1,2,0:T(8,128)}, u32[]{:S(2)}) copy-start(f32[16,128,256]{1,2,0:T(8,128)} %copy-done.2) | copy-start | bytes 6291460
  171.6 28.3 %collective-permute-start.14 = (f32[2,68,2,256]{3,2,1,0:T(2,128)}, f32[2,68,2,256]{3,2,1,0:T(2,128)S(1)}, u32[]{:S(2)}, u32[]{:S(2)}) collective-permute-start(f32[2,68,2,256]{3,2,1,0:T(2,128)} %get-tuple-element.30), channel_id=1, source_target_pairs={{0,2},{2,4},{4,6},{1,3},{3,5},{5,7},{8,10},{10,12},{12,14},{9,11},... | collective-permute-start | bytes 835592 | tf_op jit(solution)/shard_map/ppermute | solution.py:16
  173.5 26.4 %collective-permute-start.15 = (f32[2,68,2,256]{3,2,1,0:T(2,128)}, f32[2,68,2,256]{3,2,1,0:T(2,128)S(1)}, u32[]{:S(2)}, u32[]{:S(2)}) collective-permute-start(f32[2,68,2,256]{3,2,1,0:T(2,128)} %get-tuple-element.31), channel_id=1, source_target_pairs={{2,0},{4,2},{6,4},{3,1},{5,3},{7,5},{10,8},{12,10},{14,12},{11,9},... | collective-permute-start | bytes 835592 | tf_op jit(solution)/shard_map/ppermute | solution.py:19
  185.5 9.1 %collective-permute-start.10 = (f32[18,1,258]{2,0,1:T(8,128)S(1)}, f32[18,1,258]{2,0,1:T(8,128)S(1)}, u32[]{:S(2)}, u32[]{:S(2)}) collective-permute-start(f32[18,1,258]{2,0,1:T(8,128)S(1)} %copy.64), channel_id=1, source_target_pairs={{1,0},{3,2},{5,4},{7,6},{9,8},{11,10},{13,12},{15,14},{17,16},{19,... | collective-permute-start | bytes 55736 | tf_op jit(solution)/shard_map/ppermute | solution.py:19
  190.5 6.4 %collective-permute-start.11 = (f32[18,1,258]{2,0,1:T(8,128)}, f32[18,1,258]{2,0,1:T(8,128)}, u32[]{:S(2)}, u32[]{:S(2)}) collective-permute-start(f32[18,1,258]{2,0,1:T(8,128)} %copy.66), channel_id=1, source_target_pairs={{0,1},{2,3},{4,5},{6,7},{8,9},{10,11},{12,13},{14,15},{16,17},{18,... | collective-permute-start | bytes 55736 | tf_op jit(solution)/shard_map/ppermute | solution.py:16
  200.0 2.5 copy-start.5
  208.4 5.6 %copy-start.9 = (pred[256]{0:T(512)(128)(4,1)S(1)}, pred[256]{0:T(512)(128)(4,1)}, u32[]{:S(2)}) copy-start(pred[256]{0:T(512)(128)(4,1)} %copy-done.8) | copy-start | bytes 772
  208.4 20.5 %collective-permute-start.16 = (f32[2,68,36,2]{1,3,2,0:T(2,128)S(1)}, f32[2,68,36,2]{1,3,2,0:T(2,128)S(1)}, u32[]{:S(2)}, u32[]{:S(2)}) collective-permute-start(f32[2,68,36,2]{1,3,2,0:T(2,128)S(1)} %copy.71), channel_id=1, source_target_pairs={{0,1},{2,3},{4,5},{6,7},{8,9},{10,11},{12,13},{14,15},{16,17},{18,... | collective-permute-start | bytes 117512 | tf_op jit(solution)/shard_map/ppermute | solution.py:16
  212.6 19.0 %collective-permute-start.17 = (f32[2,68,36,2]{1,3,2,0:T(2,128)S(1)}, f32[2,68,36,2]{1,3,2,0:T(2,128)S(1)}, u32[]{:S(2)}, u32[]{:S(2)}) collective-permute-start(f32[2,68,36,2]{1,3,2,0:T(2,128)S(1)} %copy.72), channel_id=1, source_target_pairs={{1,0},{3,2},{5,4},{7,6},{9,8},{11,10},{13,12},{15,14},{17,16},{19,... | collective-permute-start | bytes 117512 | tf_op jit(solution)/shard_map/ppermute | solution.py:19
  245.3 0.7 copy-start.10
  245.3 0.7 copy-start.11
  245.3 0.6 copy-start.12
  245.3 0.6 copy-start.13
  245.3 0.6 copy-start.14
  246.0 8.7 %copy-start.1 = (f32[64,32,256]{2,1,0:T(8,128)S(1)}, f32[64,32,256]{2,1,0:T(8,128)}, u32[]{:S(2)}) copy-start(f32[64,32,256]{2,1,0:T(8,128)} %param.10) | copy-start | bytes 6291460
where the time goes:
time: 262 us; the launch traced here: 260 us
  local copies, waits for them, and re-layouts  108 us (41%)
  other arithmetic  92.9 us (35%)
  starting transfers between devices  57.4 us (22%)
    scatter-add x1, other arithmetic, local(): jax.ops.segment_sum(heat_flux, safe_targets, num_segments=fin_width * fin...  28.8 us
    ppermute x9, starting transfers between devices, padded_2(): lax.ppermute(lax.slice_in_dim(block, block.shape[dim] - width, None, axis...  26.2 us
    select_n x2, other arithmetic, fluid_update(): return jnp.where(update_mask, updated, field)  23.2 us
    gather x2, local copies, waits for them, and re-layouts, local(): fin_wall = jnp.where(valid, surface[safe_targets], 0.0)  23 us
    ppermute x9, starting transfers between devices, padded_2(): lax.ppermute(lax.slice_in_dim(block, 0, width, axis=dim), axis, backward)  22.7 us
    concatenate x6, other arithmetic, padded_2(): block = jnp.concatenate([low, block, high], axis=dim)  18.2 us
    slice x7, local copies, waits for them, and re-layouts, padded_2(): lax.slice_in_dim(block, 0, width, axis=dim)  17.5 us
    slice x4, local copies, waits for them, and re-layouts, padded_2(): lax.slice_in_dim(block, block.shape[dim] - width, None, axis=dim)  12.7 us
  transfers between devices with their start and end apart: 20, of which 0 were waited for; matrix products, arithmetic and copies ran while one was open for 56% of the time, Pallas kernels for 0%

commit v1 on v0

v1 whole, which is shorter than its diff:
```python
import jax
import jax.numpy as jnp
from jax import lax
from jax.experimental import pallas as pl
from jax.experimental.pallas import tpu as pltpu
from jax.sharding import PartitionSpec as P

FLUID_DIFFUSION = 1.0
FIN_CONDUCTION = 1.0
HEAT_COEF = 1.0
DIAG = 1.0 + 6.0 * FIN_CONDUCTION
SPECTRAL = 6.0 * FIN_CONDUCTION / DIAG
OMEGA = 1.0 / (1.0 - SPECTRAL * SPECTRAL / 2.0)
FLUID_SCALE = 1.0 / (1.0 + 6.0 * FLUID_DIFFUSION)
LANES = 128
PAD = 8
ROWS = 32
HIGHEST = lax.Precision.HIGHEST


def iota(shape, axis):
    return lax.broadcasted_iota(jnp.int32, shape, axis)


def tiles(value):
    return [value[:, k : k + LANES] for k in range(0, value.shape[1], LANES)]


def lane_neighbours(block, low, high):
    parts = tiles(block)
    lane = iota(parts[0].shape, 1)
    down = [pltpu.roll(part, 1, axis=1) for part in parts]
    up = [pltpu.roll(part, LANES - 1, axis=1) for part in parts]
    below = [jnp.where(lane == 0, a, b) for a, b in zip([low] + down[:-1], down)]
    above = [jnp.where(lane == LANES - 1, a, b) for a, b in zip(up[1:] + [high], up)]
    return jnp.concatenate([a + b for a, b in zip(below, above)], axis=1)


def interleave_matrix(count):
    row = iota((count, count), 0)
    col = iota((count, count), 1)
    half = count // 2
    source = jnp.where(col < half, 2 * col, 2 * (col - half) + 1)
    return (row == source).astype(jnp.float32)


def dot(a, b, contract):
    return lax.dot_general(
        a, b, (contract, ((), ())), precision=HIGHEST, preferred_element_type=jnp.float32
    )


def checker_pack(plane, parity):
    rows = plane.shape[0] // 2
    top = plane[:rows]
    bottom = plane[rows:]
    colour = (iota(top.shape, 0) + iota(top.shape, 1)) & 1
    return jnp.where(colour == parity, top, pltpu.roll(bottom, 1, axis=1))


def lane_faces(fluid, cells, rows):
    width = fluid.shape[2]
    low = jnp.zeros((rows, LANES), jnp.float32)
    high = low
    lane = iota((rows, LANES), 1)
    for i in range(cells):
        here = lane == i
        low = jnp.where(here, fluid[i + 1, PAD : PAD + rows, 0:1], low)
        high = jnp.where(here, fluid[i + 1, PAD : PAD + rows, width - 1 : width], high)
    return low.T[:cells], high.T[:cells]


def pack_faces(fluid, fin, colour, gxf, gxb, grpf, grpb, gyx, gy, dims):
    cells, rows, width, depth, fin_rows, fin_width = dims
    half = rows // 2
    inner = pl.ds(PAD, rows)
    gxf[0:half, :] = checker_pack(fluid[cells, inner, :], (colour + cells - 1) % 2)
    gxb[0:half, :] = checker_pack(fluid[1, inner, :], colour)
    low, high = lane_faces(fluid, cells, rows)
    grpf[0:cells, 0:LANES] = high
    grpb[0:cells, 0:LANES] = low
    grpf[cells : cells + fin_rows, :] = fin[depth, PAD : PAD + fin_rows, :]
    grpb[cells : cells + fin_rows, :] = fin[1, PAD : PAD + fin_rows, :]
    edge = PAD + (1 - gy) * (rows - 1)
    for i in range(cells):
        gyx[i : i + 1, :] = fluid[i + 1, pl.ds(edge, 1), :]
    lane = iota((fin_rows, LANES), 1)

    def column(d, kept):
        gxf[pl.ds(half + d, 1), :] = fin[d + 1, PAD + fin_rows - 1 : PAD + fin_rows, :]
        gxb[pl.ds(half + d, 1), :] = fin[d + 1, PAD : PAD + 1, :]
        first = fin[d + 1, PAD : PAD + fin_rows, 0:LANES]
        last = fin[d + 1, PAD : PAD + fin_rows, fin_width - LANES : fin_width]
        edge_tile = jnp.where(gy == 0, pltpu.roll(last, 1, axis=1), first)
        return jnp.where(lane == d, pltpu.roll(edge_tile, d, axis=1), kept)

    gyx[cells : cells + fin_rows, 0:LANES] = lax.fori_loop(
        0, depth, column, jnp.zeros((fin_rows, LANES), jnp.float32)
    )
    return low


def unpack_halos(fluid, fin, zlow, zhigh, hlow, hhigh, prev, nxt, below, above, side,
                 low_face, gy, prev_on, next_on, dims):
    cells, rows, width, depth, fin_rows, fin_width = dims
    half = rows // 2
    for plane, ref, on in ((0, prev, prev_on), (cells + 1, nxt, next_on)):
        packed = ref[0:half, :] * on
        fluid[plane, PAD : PAD + half, :] = packed
        fluid[plane, PAD + half : PAD + rows, :] = pltpu.roll(packed, width - 1, axis=1)
    low_on = jnp.where(gy == 0, 0.0, 1.0)
    high_on = 1.0 - low_on
    for i in range(cells):
        line = side[i : i + 1, :]
        fluid[i + 1, PAD - 1 : PAD, :] = line * low_on
        fluid[i + 1, PAD + rows : PAD + rows + 1, :] = line * high_on
    blank = jnp.zeros((LANES - cells, rows), jnp.float32)
    zlow[...] = jnp.concatenate([low_face, blank], axis=0).T
    zhigh[...] = jnp.concatenate([above[0:cells, 0:LANES], blank], axis=0).T
    fin[0, PAD : PAD + fin_rows, :] = below[cells : cells + fin_rows, :]
    fin[depth + 1, PAD : PAD + fin_rows, :] = above[cells : cells + fin_rows, :]
    columns = side[cells : cells + fin_rows, 0:LANES]
    hlow[...] = columns * low_on
    hhigh[...] = columns * high_on

    def line_of(d, carry):
        fin[d + 1, PAD - 1 : PAD, :] = prev[pl.ds(half + d, 1), :] * prev_on
        fin[d + 1, PAD + fin_rows : PAD + fin_rows + 1, :] = nxt[pl.ds(half + d, 1), :] * next_on
        return carry

    lax.fori_loop(0, depth, line_of, 0)


def fluid_sweep(fluid, active, zlow, zhigh, colour, dims, done=None):
    cells, rows, width, depth, fin_rows, fin_width = dims
    parity = (iota((ROWS, width), 0) + iota((ROWS, width), 1)) & 1

    def plane(i, carry):
        off = parity ^ ((i + colour) & 1)
        for start in range(0, rows, ROWS):
            inner = slice(PAD + start, PAD + start + ROWS)
            here = fluid[i + 1, inner, :]
            low = pltpu.roll(zlow[start : start + ROWS, :], (LANES - i) % LANES, axis=1)
            high = pltpu.roll(zhigh[start : start + ROWS, :], LANES - 1 - i, axis=1)
            total = (
                fluid[i, inner, :]
                + fluid[i + 2, inner, :]
                + fluid[i + 1, PAD + start - 1 : PAD + start + ROWS - 1, :]
                + fluid[i + 1, PAD + start + 1 : PAD + start + ROWS + 1, :]
                + lane_neighbours(here, low, high)
            )
            updated = (here + FLUID_DIFFUSION * total) * FLUID_SCALE
            mask = active[i, start : start + ROWS, :] > off
            fluid[i + 1, inner, :] = jnp.where(mask, updated, here)
        if done is not None:
            done(i)
        return carry

    lax.fori_loop(0, cells, plane, 0)


def fin_neighbours(fin, d, hlow, hhigh, fin_rows):
    inner = slice(PAD, PAD + fin_rows)
    here = fin[d + 1, inner, :]
    low = pltpu.roll(hlow[...], (LANES - d) % LANES, axis=1)
    high = pltpu.roll(hhigh[...], LANES - 1 - d, axis=1)
    total = (
        fin[d, inner, :]
        + fin[d + 2, inner, :]
        + fin[d + 1, PAD - 1 : PAD + fin_rows - 1, :]
        + fin[d + 1, PAD + 1 : PAD + fin_rows + 1, :]
        + lane_neighbours(here, low, high)
    )
    return here, total


def solution(mesh):
    in_specs = (
        P("gx", "gy", "grp"),
        P("gx", "gy", "grp"),
        P("grp", "gx", "gy"),
        P("grp", "gx", "gy"),
        P("gx", "gy", None, None),
        P("gx", "gy", None),
    )
    out_specs = (P("gx", "gy", "grp"), P("grp", "gx", "gy"))
    count = mesh.shape["gx"]
    groups = mesh.shape["grp"]
    sides = mesh.shape["gy"]
    assert sides == 2
    ring = count == 4
    vmem = pl.BlockSpec(memory_space=pltpu.VMEM)
    hbm = pl.BlockSpec(memory_space=pl.ANY)

    def local(fluid_temp, active, fin_temp, fin_source, wall_owner, wall_target):
        cells, rows, width = fluid_temp.shape
        depth, fin_rows, fin_width = fin_temp.shape
        assert rows == LANES and width == fin_width == 2 * rows and fin_rows == 2 * cells
        assert depth <= LANES and cells % 2 == 0 and rows % ROWS == 0 and fin_rows == ROWS
        dims = (cells, rows, width, depth, fin_rows, fin_width)
        half = rows // 2
        face_rows = half + depth
        wall_rows = fin_rows + cells
        small_rows = cells + fin_rows
        gx_rows = face_rows + (wall_rows if ring else 0)
        owners = wall_owner.reshape(cells, rows)
        targets = wall_target.reshape(cells, rows)
        f32 = lambda *shape: jax.ShapeDtypeStruct(shape, jnp.float32)
        params = pltpu.CompilerParams(vmem_limit_bytes=32 * 1024 * 1024)
        fluid_pad = f32(cells + 2, rows + 2 * PAD, width)
        fin_pad = f32(depth + 2, fin_rows + 2 * PAD, fin_width)
        faces = (f32(small_rows, width), f32(small_rows, width), f32(small_rows, width))

        def start_kernel(fluid_hbm, fin_hbm, own, tgt, fluid, fin, gxf, gxb, grpf, grpb, gyx,
                         wall, sems):
            copies = (
                pltpu.make_async_copy(
                    fluid_hbm, fluid.at[pl.ds(1, cells), pl.ds(PAD, rows), :], sems.at[0]
                ),
                pltpu.make_async_copy(
                    fin_hbm, fin.at[pl.ds(1, depth), pl.ds(PAD, fin_rows), :], sems.at[1]
                ),
            )
            for copy in copies:
                copy.start()
            gy = lax.axis_index("gy")
            shape = (cells, rows)
            shift = tgt[...] - 2 * (iota(shape, 0) * fin_width + iota(shape, 1))
            row_shift = (shift >= fin_width).astype(jnp.int32)
            code = own[...] * 4 + row_shift * 2 + (shift - row_shift * fin_width)
            wall[fin_rows:, LANES:] = code.astype(jnp.float32)
            for copy in copies:
                copy.wait()
            bottom = pack_faces(fluid, fin, 1, gxf, gxb, grpf, grpb, gyx, gy, dims)
            wall[fin_rows:, 0:LANES] = bottom
            surface = fin[1, PAD : PAD + fin_rows, :]
            even_rows = dot(interleave_matrix(fin_rows), surface, ((0,), (0,)))
            wall[0:fin_rows, :] = dot(even_rows, interleave_matrix(fin_width), ((1,), (0,)))
            if ring:
                gxf[face_rows:, :] = wall[...]
                gxb[face_rows:, :] = wall[...]

        fluid0, fin0, gxf, gxb, grpf, grpb, gyx, wall = pl.pallas_call(
            start_kernel,
            out_shape=(fluid_pad, fin_pad, f32(gx_rows, width), f32(gx_rows, width)) + faces
            + (f32(wall_rows, width),),
            in_specs=[hbm, hbm, vmem, vmem],
            out_specs=(vmem,) * 8,
            scratch_shapes=[pltpu.SemaphoreType.DMA((2,))],
            compiler_params=params,
            name="start",
        )(fluid_temp, fin_temp, owners, targets)

        def chain(size, step):
            return [(i, i + step) for i in range(size) if 0 <= i + step < size]

        def around(size, step):
            return [(i, (i + step) % size) for i in range(size)]

        swap = [(0, 1), (1, 0)]
        if ring:
            prev = lax.ppermute(gxf, "gx", around(count, 1))
            nxt = lax.ppermute(gxb, "gx", around(count, -1))
            walls = [wall] + [lax.ppermute(wall, "gx", around(count, k)) for k in range(2, count - 1)]
        else:
            prev = lax.ppermute(gxf, "gx", chain(count, 1))
            nxt = lax.ppermute(gxb, "gx", chain(count, -1))
            walls = [wall, lax.all_gather(wall, "gx")]
        below = lax.ppermute(grpf, "grp", chain(groups, 1))
        above = lax.ppermute(grpb, "grp", chain(groups, -1))
        side = lax.ppermute(gyx, "gy", swap)

        def middle_kernel(*refs):
            (act, prev, nxt, below, above, side), refs = (refs[2],) + refs[4:9], refs[9:]
            wall_refs, refs = refs[: len(walls)], refs[len(walls) :]
            fluid, fin, first, src, ghost_out, gxf, gxb, grpf, grpb, gyx = refs[:10]
            zlow, zhigh, hlow, hhigh = refs[10:]
            gx = lax.axis_index("gx")
            gy = lax.axis_index("gy")
            on_wall = lax.axis_index("grp") == 0
            own = wall_refs[0]
            own_code = own[fin_rows:, LANES:]
            if ring:
                slots = [(gx, own, 0), ((gx + count - 1) % count, prev, face_rows),
                         ((gx + 1) % count, nxt, face_rows)]
                slots += [((gx + count - k) % count, ref, 0) for k, ref in
                          zip(range(2, count - 1), wall_refs[1:])]
                slots = [(o, ref.at[pl.ds(base, wall_rows), :]) for o, ref, base in slots]
            else:
                slots = [(s, wall_refs[1].at[s]) for s in range(count)]
            quadrants = [(a * cells, b * LANES) for a in range(2) for b in range(2)]
            ghost = jnp.zeros((cells, rows), jnp.float32)
            deposits = [jnp.zeros((cells, rows), jnp.float32) for _ in quadrants]
            mine = (4 * gx).astype(jnp.float32)
            for owner, ref in slots:
                theirs = own_code - (4 * jnp.asarray(owner, jnp.int32)).astype(jnp.float32)
                temps = ref[fin_rows:, 0:LANES]
                wanted = ref[fin_rows:, LANES:] - mine
                for q, (r, c) in enumerate(quadrants):
                    ghost = jnp.where(theirs == q, ref[r : r + cells, c : c + LANES], ghost)
                    flux = HEAT_COEF * (temps - own[r : r + cells, c : c + LANES])
                    deposits[q] = deposits[q] + jnp.where(wanted == q, flux, 0.0)
            ghost_out[...] = ghost

            @pl.when(on_wall)
            def _():
                split = jnp.concatenate(
                    [jnp.concatenate(deposits[0:2], axis=1), jnp.concatenate(deposits[2:4], axis=1)],
                    axis=0,
                )
                mixed = dot(split, interleave_matrix(fin_width), ((1,), (1,)))
                src[0] = src[0] + dot(interleave_matrix(fin_rows), mixed, ((1,), (0,)))

            low_face = jnp.where(on_wall, ghost, below[0:cells, 0:LANES])
            prev_on = jnp.where(gx == 0, 0.0, 1.0)
            next_on = jnp.where(gx == count - 1, 0.0, 1.0)
            unpack_halos(fluid, fin, zlow, zhigh, hlow, hhigh, prev, nxt, below, above, side,
                         low_face, gy, prev_on, next_on, dims)
            fluid_sweep(fluid, act, zlow, zhigh, 0, dims)

            def layer(d, carry):
                here, total = fin_neighbours(fin, d, hlow, hhigh, fin_rows)
                rhs = here + src[d]
                first[d + 1, PAD : PAD + fin_rows, :] = (rhs + FIN_CONDUCTION * total) * (1.0 / DIAG)
                src[d] = rhs * (OMEGA / DIAG) + here * (1.0 - OMEGA)
                return carry

            lax.fori_loop(0, depth, layer, 0)
            pack_faces(fluid, first, 0, gxf, gxb, grpf, grpb, gyx, gy, dims)

        received = (prev, nxt, below, above, side)
        scratch = [
            pltpu.VMEM((rows, LANES), jnp.float32),
            pltpu.VMEM((rows, LANES), jnp.float32),
            pltpu.VMEM((fin_rows, LANES), jnp.float32),
            pltpu.VMEM((fin_rows, LANES), jnp.float32),
        ]
        outs = pl.pallas_call(
            middle_kernel,
            out_shape=(fluid_pad, fin_pad, fin_pad, f32(depth, fin_rows, fin_width),
                       f32(cells, rows), f32(face_rows, width), f32(face_rows, width)) + faces,
            in_specs=[vmem] * (9 + len(walls)),
            out_specs=(vmem,) * 10,
            scratch_shapes=scratch,
            input_output_aliases={0: 0, 1: 1, 3: 3},
            compiler_params=params,
            name="middle",
        )(fluid0, fin0, active, fin_source, *received, *walls)
        fluid1, _, first, rest, ghost, gxf, gxb, grpf, grpb, gyx = outs

        prev = lax.ppermute(gxf, "gx", chain(count, 1))
        nxt = lax.ppermute(gxb, "gx", chain(count, -1))
        below = lax.ppermute(grpf, "grp", chain(groups, 1))
        above = lax.ppermute(grpb, "grp", chain(groups, -1))
        side = lax.ppermute(gyx, "gy", swap)

        def end_kernel(_0, _1, _2, act, ghost, prev, nxt, below, above, side,
                       fluid, first, rest, fluid_new, fin_new,
                       zlow, zhigh, hlow, hhigh, fluid_sems, fin_sems):
            gy = lax.axis_index("gy")
            on_wall = lax.axis_index("grp") == 0
            low_face = jnp.where(on_wall, ghost[...], below[0:cells, 0:LANES])
            unpack_halos(fluid, first, zlow, zhigh, hlow, hhigh, prev, nxt, below, above, side,
                         low_face, gy, 1.0, 1.0, dims)

            def fluid_copy(i):
                return pltpu.make_async_copy(
                    fluid.at[i + 1, pl.ds(PAD, rows), :], fluid_new.at[i], fluid_sems.at[i]
                )

            def fin_copy(d):
                return pltpu.make_async_copy(rest.at[d], fin_new.at[d], fin_sems.at[d])

            fluid_sweep(fluid, act, zlow, zhigh, 1, dims, lambda i: fluid_copy(i).start())

            def layer(d, carry):
                _, total = fin_neighbours(first, d, hlow, hhigh, fin_rows)
                rest[d] = rest[d] + (OMEGA * FIN_CONDUCTION / DIAG) * total
                fin_copy(d).start()
                return carry

            lax.fori_loop(0, depth, layer, 0)

            def finish_fluid(i, carry):
                fluid_copy(i).wait()
                return carry

            def finish_fin(d, carry):
                fin_copy(d).wait()
                return carry

            lax.fori_loop(0, cells, finish_fluid, 0)
            lax.fori_loop(0, depth, finish_fin, 0)

        results = pl.pallas_call(
            end_kernel,
            out_shape=(fluid_pad, fin_pad, f32(depth, fin_rows, fin_width),
                       f32(cells, rows, width), f32(depth, fin_rows, fin_width)),
            in_specs=[vmem] * 10,
            out_specs=(vmem, vmem, vmem, hbm, hbm),
            scratch_shapes=scratch + [pltpu.SemaphoreType.DMA((cells,)),
                                      pltpu.SemaphoreType.DMA((depth,))],
            input_output_aliases={0: 0, 1: 1, 2: 2},
            compiler_params=params,
            name="end",
        )(fluid1, first, rest, active, ghost, prev, nxt, below, above, side)
        return results[3], results[4]

    return jax.shard_map(local, mesh=mesh, in_specs=in_specs, out_specs=out_specs, check_vma=False)
```

time: 262 us -> 76.6 us (0.29)
  local copies, waits for them, and re-layouts: 108 us -> 4.23 us
  other arithmetic: 92.9 us -> 0 us
  Pallas kernels: 0 us -> 42 us
  starting transfers between devices: 57.4 us -> 22.1 us
  waiting for transfers between devices: 0.05 us -> 7.19 us
    pallas_call x0 -> x3, Pallas kernels: none -> 42 us  [the longest x1 19.9 us: local(): pl.pallas_call(middle_kernel, out_shape=(fluid_pad, fin_pad, fin_pad, f32...]
    gather x3 -> x0, local copies, waits for them, and re-layouts: 34.8 us -> none  [the longest x2 23 us: local(): fin_wall = jnp.where(valid, surface[safe_targets], 0.0)]
    select_n x7 -> x0, other arithmetic: 32 us -> none  [the longest x2 23.2 us: fluid_update(): return jnp.where(update_mask, updated, field)]
    slice x11 -> x0, local copies, waits for them, and re-layouts: 30.2 us -> none  [the longest x7 17.5 us: padded_2(): lax.slice_in_dim(block, 0, width, axis=dim)]
    scatter-add x2 -> x0, other arithmetic: 28.8 us -> none  [the longest x1 28.8 us: local(): jax.ops.segment_sum(heat_flux, safe_targets, num_segments=fin_width * fin...]
    ppermute x18 -> x11, starting transfers between devices: 48.9 us -> 22.1 us  [the longest x2 6.96 us: local(): below = lax.ppermute(grpf, 'grp', chain(groups, 1))]
    concatenate x6 -> x0, other arithmetic: 18.2 us -> none  [padded_2(): block = jnp.concatenate([low, block, high], axis=dim)]
    scatter x2 -> x0, local copies, waits for them, and re-layouts: 16.1 us -> none  [the longest x1 8.06 us: local(): jnp.zeros((owner_count * capacity,), jnp.float32).at[slot_index]]
  transfers between devices with their start and end apart: 20 -> 11, of which waited for: 0 -> 3; matrix products, arithmetic and copies ran while one was open for 56% -> 0% of each run, Pallas kernels for 0% -> 0%
where the time goes in v1:
time: 76.6 us; the launch traced here: 76.3 us
  Pallas kernels  42 us (55%)
  starting transfers between devices  22.1 us (29%)
  waiting for transfers between devices  7.19 us (9%)
  local copies, waits for them, and re-layouts  4.23 us (6%)
    pallas_call x1, Pallas kernels, local(): pl.pallas_call(middle_kernel, out_shape=(fluid_pad, fin_pad, fin_pad, f32...  19.9 us
    pallas_call x1, Pallas kernels, local(): pl.pallas_call(end_kernel, out_shape=(fluid_pad, fin_pad, f32(depth, fin_...  11.4 us
    pallas_call x1, Pallas kernels, local(): pl.pallas_call(start_kernel, out_shape=(fluid_pad, fin_pad, f32(gx_rows,...  10.8 us
    ppermute x2, starting transfers between devices, local(): below = lax.ppermute(grpf, 'grp', chain(groups, 1))  6.96 us
    ppermute x2, waiting for transfers between devices, local(): above = lax.ppermute(grpb, 'grp', chain(groups, -1))  6.45 us
    ppermute x2, starting transfers between devices, local(): above = lax.ppermute(grpb, 'grp', chain(groups, -1))  4.71 us
    ppermute x1, starting transfers between devices, local(): nxt = lax.ppermute(gxb, 'gx', chain(count, -1))  4.24 us
    unnamed x11, local copies, waits for them, and re-layouts  4.23 us
  transfers between devices with their start and end apart: 11, of which 3 were waited for; matrix products, arithmetic and copies ran while one was open for 0% of the time, Pallas kernels for 0%

profile of v1, /device:TPU:12, one launch (start us, length us, event | category | flops | bytes accessed | tf_op | source)
XLA Modules:
  0.0 76.3 jit_solution(18365574369877393156)
XLA Ops:
  0.6 0.0 copy-start.1
  0.6 0.0 copy-start.2
  0.6 1.7 %copy.21.refs_3_ = f32[64,32,256]{2,1,0:T(8,128)S(1)} copy(f32[64,32,256]{2,1,0:T(8,128)} %param.9) | data formatting | bytes 4194304
  2.4 0.5 copy-done.1
  2.9 0.6 copy-done.2
  3.5 0.0 copy-start.3
  3.5 0.7 copy-done.3
  4.2 0.0 copy-start.4
  4.2 0.7 copy-done.4
  4.9 0.0 copy-start
  4.9 10.8 %start.1 = (f32[18,144,256]{2,1,0:T(8,128)S(1)}, f32[66,48,256]{2,1,0:T(8,128)S(1)}, f32[176,256]{1,0:T(8,128)S(1)}, f32[176,256]{1,0:T(8,128)S(1)}, f32[48,256]...) custom-call(f32[16,128,256]{2,1,0:T(8,128)S(1)} %copy-done.1, ...), custom_call_target="tpu_custom_call" | custom-call | tf_op jit(solution)/shard_map/start/pallas_call | solution.py:243
  15.7 1.5 %collective-permute-start = (f32[176,256]{1,0:T(8,128)S(1)}, f32[176,256]{1,0:T(8,128)S(1)}, u32[]{:S(2)}, u32[]{:S(2)}) collective-permute-start(f32[176,256]{1,0:T(8,128)S(1)} %get-tuple-element.23), channel_id=1, source_target_pairs={{0,2},{2,4},{4,6},{6,0},{1,3},{3,5},{5,7},{7,1},{8,10},{10,12},{12... | collective-permute-start | bytes 540680 | tf_op jit(solution)/shard_map/ppermute | solution.py:262
  17.2 1.4 %collective-permute-start.1 = (f32[176,256]{1,0:T(8,128)S(1)}, f32[176,256]{1,0:T(8,128)S(1)}, u32[]{:S(2)}, u32[]{:S(2)}) collective-permute-start(f32[176,256]{1,0:T(8,128)S(1)} %get-tuple-element.24), channel_id=1, source_target_pairs={{0,6},{2,0},{4,2},{6,4},{1,7},{3,1},{5,3},{7,5},{8,14},{10,8},{12,... | collective-permute-start | bytes 540680 | tf_op jit(solution)/shard_map/ppermute | solution.py:263
  18.6 3.5 %collective-permute-start.2 = (f32[48,256]{1,0:T(8,128)S(1)}, f32[48,256]{1,0:T(8,128)S(1)}, u32[]{:S(2)}, u32[]{:S(2)}) collective-permute-start(f32[48,256]{1,0:T(8,128)S(1)} %get-tuple-element.25), channel_id=1, source_target_pairs={{0,8},{8,16},{16,24},{1,9},{9,17},{17,25},{2,10},{10,18},{18,26},{... | collective-permute-start | bytes 147464 | tf_op jit(solution)/shard_map/ppermute | solution.py:269
  22.1 2.4 %collective-permute-start.3 = (f32[48,256]{1,0:T(8,128)S(1)}, f32[48,256]{1,0:T(8,128)S(1)}, u32[]{:S(2)}, u32[]{:S(2)}) collective-permute-start(f32[48,256]{1,0:T(8,128)S(1)} %get-tuple-element.26), channel_id=1, source_target_pairs={{8,0},{16,8},{24,16},{9,1},{17,9},{25,17},{10,2},{18,10},{26,18},{... | collective-permute-start | bytes 147464 | tf_op jit(solution)/shard_map/ppermute | solution.py:270
  24.5 0.1 collective-permute-start.4
  24.6 0.0 collective-permute-done.2.refs_6_
  24.6 0.5 collective-permute-start.5
  25.1 3.0 %collective-permute-done.3.refs_7_ = f32[48,256]{1,0:T(8,128)S(1)} collective-permute-done((f32[48,256]{1,0:T(8,128)S(1)}, f32[48,256]{1,0:T(8,128)S(1)}, u32[]{:S(2)}, u32[]{:S(2)}) %collective-permute-start.3) | collective-permute-done | bytes 49184 | tf_op jit(solution)/shard_map/ppermute | solution.py:270
  28.1 0.0 collective-permute-done.4.refs_8_
  28.1 0.6 collective-permute-done.5.refs_10_
  28.7 0.0 collective-permute-done.refs_4_
  28.7 0.0 collective-permute-done.1.refs_5_
  28.7 0.0 copy-done
  28.7 19.9 %middle.1 = (f32[18,144,256]{2,1,0:T(8,128)S(1)}, f32[66,48,256]{2,1,0:T(8,128)S(1)}, f32[66,48,256]{2,1,0:T(8,128)S(1)}, f32[64,32,256]{2,1,0:T(8,128)S(1)}, f3...) custom-call(f32[18,144,256]{2,1,0:T(8,128)S(1)} %get-tuple-element.2, ...), custom_call_target="tpu_custom_call", output_to_operand_aliasing={{0}: (0, {}), {1}: (1, {}), {3}: (3, {})} | custom-call | tf_op jit(solution)/shard_map/middle/pallas_call | solution.py:338
  48.6 2.6 %collective-permute-start.6 = (f32[128,256]{1,0:T(8,128)S(1)}, f32[128,256]{1,0:T(8,128)S(1)}, u32[]{:S(2)}, u32[]{:S(2)}) collective-permute-start(f32[128,256]{1,0:T(8,128)S(1)} %get-tuple-element.33), channel_id=1, source_target_pairs={{0,2},{2,4},{4,6},{1,3},{3,5},{5,7},{8,10},{10,12},{12,14},{9,11},... | collective-permute-start | bytes 393224 | tf_op jit(solution)/shard_map/ppermute | solution.py:351
  51.2 4.2 %collective-permute-start.7 = (f32[128,256]{1,0:T(8,128)S(1)}, f32[128,256]{1,0:T(8,128)S(1)}, u32[]{:S(2)}, u32[]{:S(2)}) collective-permute-start(f32[128,256]{1,0:T(8,128)S(1)} %get-tuple-element.34), channel_id=1, source_target_pairs={{2,0},{4,2},{6,4},{3,1},{5,3},{7,5},{10,8},{12,10},{14,12},{11,9},... | collective-permute-start | bytes 393224 | tf_op jit(solution)/shard_map/ppermute | solution.py:352
  55.4 3.5 %collective-permute-start.8 = (f32[48,256]{1,0:T(8,128)S(1)}, f32[48,256]{1,0:T(8,128)S(1)}, u32[]{:S(2)}, u32[]{:S(2)}) collective-permute-start(f32[48,256]{1,0:T(8,128)S(1)} %get-tuple-element.35), channel_id=1, source_target_pairs={{0,8},{8,16},{16,24},{1,9},{9,17},{17,25},{2,10},{10,18},{18,26},{... | collective-permute-start | bytes 147464 | tf_op jit(solution)/shard_map/ppermute | solution.py:353
  58.9 2.4 %collective-permute-start.9 = (f32[48,256]{1,0:T(8,128)S(1)}, f32[48,256]{1,0:T(8,128)S(1)}, u32[]{:S(2)}, u32[]{:S(2)}) collective-permute-start(f32[48,256]{1,0:T(8,128)S(1)} %get-tuple-element.36), channel_id=1, source_target_pairs={{8,0},{16,8},{24,16},{9,1},{17,9},{25,17},{10,2},{18,10},{26,18},{... | collective-permute-start | bytes 147464 | tf_op jit(solution)/shard_map/ppermute | solution.py:354
  61.3 0.1 collective-permute-start.10
  61.4 0.0 collective-permute-done.8.below
  61.4 3.5 %collective-permute-done.9.above = f32[48,256]{1,0:T(8,128)S(1)} collective-permute-done((f32[48,256]{1,0:T(8,128)S(1)}, f32[48,256]{1,0:T(8,128)S(1)}, u32[]{:S(2)}, u32[]{:S(2)}) %collective-permute-start.9) | collective-permute-done | bytes 49184 | tf_op jit(solution)/shard_map/ppermute | solution.py:354
  64.9 0.0 collective-permute-done.10.side
  64.9 0.0 collective-permute-done.6.prev
  64.9 0.0 collective-permute-done.7.nxt
  64.9 11.4 %end.1 = (f32[18,144,256]{2,1,0:T(8,128)S(1)}, f32[66,48,256]{2,1,0:T(8,128)S(1)}, f32[64,32,256]{2,1,0:T(8,128)S(1)}, f32[16,128,256]{2,1,0:T(8,128)}, f32[64,32,256]{2,1,0:T(8,128)}) custom-call(f32[18,144,256]{2,1,0:T(8,128)S(1)} %get-tuple-element.29._0, ...), custom_call_target="tpu_custom_call", output_to_operand_aliasing={{0}: (0, {}), {1}: (1, {}), {2}: (2, {})} | custom-call | tf_op jit(solution)/shard_map/end/pallas_call | solution.py:395
Async XLA Ops:
  0.6 2.2 %copy-start.1 = (f32[16,128,256]{2,1,0:T(8,128)S(1)}, f32[16,128,256]{2,1,0:T(8,128)}, u32[]{:S(2)}) copy-start(f32[16,128,256]{2,1,0:T(8,128)} %fluid_hbm.1) | copy-start | bytes 6291460
  0.6 2.8 %copy-start.2 = (f32[64,32,256]{2,1,0:T(8,128)S(1)}, f32[64,32,256]{2,1,0:T(8,128)}, u32[]{:S(2)}) copy-start(f32[64,32,256]{2,1,0:T(8,128)} %fin_hbm.1) | copy-start | bytes 6291460
  3.5 0.7 copy-start.3
  4.2 0.7 copy-start.4
  4.9 23.8 %copy-start = (s32[16,128,256]{2,1,0:T(8,128)S(1)}, s32[16,128,256]{2,1,0:T(8,128)}, u32[]{:S(2)}) copy-start(s32[16,128,256]{2,1,0:T(8,128)} %act.1) | copy-start | bytes 6291460
  15.7 13.1 %collective-permute-start = (f32[176,256]{1,0:T(8,128)S(1)}, f32[176,256]{1,0:T(8,128)S(1)}, u32[]{:S(2)}, u32[]{:S(2)}) collective-permute-start(f32[176,256]{1,0:T(8,128)S(1)} %get-tuple-element.23), channel_id=1, source_target_pairs={{0,2},{2,4},{4,6},{6,0},{1,3},{3,5},{5,7},{7,1},{8,10},{10,12},{12... | collective-permute-start | bytes 540680 | tf_op jit(solution)/shard_map/ppermute | solution.py:262
  17.2 11.5 %collective-permute-start.1 = (f32[176,256]{1,0:T(8,128)S(1)}, f32[176,256]{1,0:T(8,128)S(1)}, u32[]{:S(2)}, u32[]{:S(2)}) collective-permute-start(f32[176,256]{1,0:T(8,128)S(1)} %get-tuple-element.24), channel_id=1, source_target_pairs={{0,6},{2,0},{4,2},{6,4},{1,7},{3,1},{5,3},{7,5},{8,14},{10,8},{12,... | collective-permute-start | bytes 540680 | tf_op jit(solution)/shard_map/ppermute | solution.py:263
  18.6 6.0 %collective-permute-start.2 = (f32[48,256]{1,0:T(8,128)S(1)}, f32[48,256]{1,0:T(8,128)S(1)}, u32[]{:S(2)}, u32[]{:S(2)}) collective-permute-start(f32[48,256]{1,0:T(8,128)S(1)} %get-tuple-element.25), channel_id=1, source_target_pairs={{0,8},{8,16},{16,24},{1,9},{9,17},{17,25},{2,10},{10,18},{18,26},{... | collective-permute-start | bytes 147464 | tf_op jit(solution)/shard_map/ppermute | solution.py:269
  22.1 6.0 %collective-permute-start.3 = (f32[48,256]{1,0:T(8,128)S(1)}, f32[48,256]{1,0:T(8,128)S(1)}, u32[]{:S(2)}, u32[]{:S(2)}) collective-permute-start(f32[48,256]{1,0:T(8,128)S(1)} %get-tuple-element.26), channel_id=1, source_target_pairs={{8,0},{16,8},{24,16},{9,1},{17,9},{25,17},{10,2},{18,10},{26,18},{... | collective-permute-start | bytes 147464 | tf_op jit(solution)/shard_map/ppermute | solution.py:270
  24.5 3.6 %collective-permute-start.4 = (f32[48,256]{1,0:T(8,128)S(1)}, f32[48,256]{1,0:T(8,128)S(1)}, u32[]{:S(2)}, u32[]{:S(2)}) collective-permute-start(f32[48,256]{1,0:T(8,128)S(1)} %get-tuple-element.27), channel_id=1, source_target_pairs={{0,1},{1,0},{2,3},{3,2},{4,5},{5,4},{6,7},{7,6},{8,9},{9,8},{10,11... | collective-permute-start | bytes 147464 | tf_op jit(solution)/shard_map/ppermute | solution.py:271
  24.6 4.1 %collective-permute-start.5 = (f32[48,256]{1,0:T(8,128)S(1)}, f32[48,256]{1,0:T(8,128)S(1)}, u32[]{:S(2)}, u32[]{:S(2)}) collective-permute-start(f32[48,256]{1,0:T(8,128)S(1)} %get-tuple-element.28.refs_9_), channel_id=1, source_target_pairs={{0,4},{2,6},{4,0},{6,2},{1,5},{3,7},{5,1},{7,3},{8,12},{10,14},{12... | collective-permute-start | bytes 147464 | tf_op jit(solution)/shard_map/ppermute | solution.py:264
  48.6 16.3 %collective-permute-start.6 = (f32[128,256]{1,0:T(8,128)S(1)}, f32[128,256]{1,0:T(8,128)S(1)}, u32[]{:S(2)}, u32[]{:S(2)}) collective-permute-start(f32[128,256]{1,0:T(8,128)S(1)} %get-tuple-element.33), channel_id=1, source_target_pairs={{0,2},{2,4},{4,6},{1,3},{3,5},{5,7},{8,10},{10,12},{12,14},{9,11},... | collective-permute-start | bytes 393224 | tf_op jit(solution)/shard_map/ppermute | solution.py:351
  51.2 13.7 %collective-permute-start.7 = (f32[128,256]{1,0:T(8,128)S(1)}, f32[128,256]{1,0:T(8,128)S(1)}, u32[]{:S(2)}, u32[]{:S(2)}) collective-permute-start(f32[128,256]{1,0:T(8,128)S(1)} %get-tuple-element.34), channel_id=1, source_target_pairs={{2,0},{4,2},{6,4},{3,1},{5,3},{7,5},{10,8},{12,10},{14,12},{11,9},... | collective-permute-start | bytes 393224 | tf_op jit(solution)/shard_map/ppermute | solution.py:352
  55.4 6.0 %collective-permute-start.8 = (f32[48,256]{1,0:T(8,128)S(1)}, f32[48,256]{1,0:T(8,128)S(1)}, u32[]{:S(2)}, u32[]{:S(2)}) collective-permute-start(f32[48,256]{1,0:T(8,128)S(1)} %get-tuple-element.35), channel_id=1, source_target_pairs={{0,8},{8,16},{16,24},{1,9},{9,17},{17,25},{2,10},{10,18},{18,26},{... | collective-permute-start | bytes 147464 | tf_op jit(solution)/shard_map/ppermute | solution.py:353
  58.9 6.0 %collective-permute-start.9 = (f32[48,256]{1,0:T(8,128)S(1)}, f32[48,256]{1,0:T(8,128)S(1)}, u32[]{:S(2)}, u32[]{:S(2)}) collective-permute-start(f32[48,256]{1,0:T(8,128)S(1)} %get-tuple-element.36), channel_id=1, source_target_pairs={{8,0},{16,8},{24,16},{9,1},{17,9},{25,17},{10,2},{18,10},{26,18},{... | collective-permute-start | bytes 147464 | tf_op jit(solution)/shard_map/ppermute | solution.py:354
  61.3 3.6 %collective-permute-start.10 = (f32[48,256]{1,0:T(8,128)S(1)}, f32[48,256]{1,0:T(8,128)S(1)}, u32[]{:S(2)}, u32[]{:S(2)}) collective-permute-start(f32[48,256]{1,0:T(8,128)S(1)} %get-tuple-element.37), channel_id=1, source_target_pairs={{0,1},{1,0},{2,3},{3,2},{4,5},{5,4},{6,7},{7,6},{8,9},{9,8},{10,11... | collective-permute-start | bytes 147464 | tf_op jit(solution)/shard_map/ppermute | solution.py:355

commit v2 on v1

--- a/solution.py
+++ b/solution.py
@@ -20,6 +20,15 @@
 
 def iota(shape, axis):
     return lax.broadcasted_iota(jnp.int32, shape, axis)
+
+
+def repeat(count, body, step=8):
+    def trip(k, carry):
+        for j in range(step):
+            body(k * step + j)
+        return carry
+
+    lax.fori_loop(0, count // step, trip, 0)
 
 
 def tiles(value):
@@ -86,17 +95,25 @@
         gyx[i : i + 1, :] = fluid[i + 1, pl.ds(edge, 1), :]
     lane = iota((fin_rows, LANES), 1)
 
-    def column(d, kept):
+    def columns(at):
+        kept = jnp.zeros((fin_rows, LANES), jnp.float32)
+        for d in range(depth):
+            kept = jnp.where(lane == d, fin[d + 1, PAD : PAD + fin_rows, at : at + 1], kept)
+        gyx[cells : cells + fin_rows, 0:LANES] = kept
+
+    @pl.when(gy == 0)
+    def _():
+        columns(fin_width - 1)
+
+    @pl.when(gy != 0)
+    def _():
+        columns(0)
+
+    def lines(d):
         gxf[pl.ds(half + d, 1), :] = fin[d + 1, PAD + fin_rows - 1 : PAD + fin_rows, :]
         gxb[pl.ds(half + d, 1), :] = fin[d + 1, PAD : PAD + 1, :]
-        first = fin[d + 1, PAD : PAD + fin_rows, 0:LANES]
-        last = fin[d + 1, PAD : PAD + fin_rows, fin_width - LANES : fin_width]
-        edge_tile = jnp.where(gy == 0, pltpu.roll(last, 1, axis=1), first)
-        return jnp.where(lane == d, pltpu.roll(edge_tile, d, axis=1), kept)
-
-    gyx[cells : cells + fin_rows, 0:LANES] = lax.fori_loop(
-        0, depth, column, jnp.zeros((fin_rows, LANES), jnp.float32)
-    )
+
+    repeat(depth, lines)
     return low
 
 
@@ -123,12 +140,11 @@
     hlow[...] = columns * low_on
     hhigh[...] = columns * high_on
 
-    def line_of(d, carry):
+    def line_of(d):
         fin[d + 1, PAD - 1 : PAD, :] = prev[pl.ds(half + d, 1), :] * prev_on
         fin[d + 1, PAD + fin_rows : PAD + fin_rows + 1, :] = nxt[pl.ds(half + d, 1), :] * next_on
-        return carry
-
-    lax.fori_loop(0, depth, line_of, 0)
+
+    repeat(depth, line_of)
 
 
 def fluid_sweep(fluid, active, zlow, zhigh, colour, dims, done=None):
@@ -196,7 +212,7 @@
         cells, rows, width = fluid_temp.shape
         depth, fin_rows, fin_width = fin_temp.shape
         assert rows == LANES and width == fin_width == 2 * rows and fin_rows == 2 * cells
-        assert depth <= LANES and cells % 2 == 0 and rows % ROWS == 0 and fin_rows == ROWS
+        assert depth <= LANES and depth % 8 == 0 and cells % 2 == 0 and rows % ROWS == 0 and fin_rows == ROWS
         dims = (cells, rows, width, depth, fin_rows, fin_width)
         half = rows // 2
         face_rows = half + depth
@@ -318,14 +334,13 @@
                          low_face, gy, prev_on, next_on, dims)
             fluid_sweep(fluid, act, zlow, zhigh, 0, dims)
 
-            def layer(d, carry):
+            def layer(d):
                 here, total = fin_neighbours(fin, d, hlow, hhigh, fin_rows)
                 rhs = here + src[d]
                 first[d + 1, PAD : PAD + fin_rows, :] = (rhs + FIN_CONDUCTION * total) * (1.0 / DIAG)
                 src[d] = rhs * (OMEGA / DIAG) + here * (1.0 - OMEGA)
-                return carry
-
-            lax.fori_loop(0, depth, layer, 0)
+
+            repeat(depth, layer)
             pack_faces(fluid, first, 0, gxf, gxb, grpf, grpb, gyx, gy, dims)
 
         received = (prev, nxt, below, above, side)
@@ -368,18 +383,21 @@
                     fluid.at[i + 1, pl.ds(PAD, rows), :], fluid_new.at[i], fluid_sems.at[i]
                 )
 
-            def fin_copy(d):
-                return pltpu.make_async_copy(rest.at[d], fin_new.at[d], fin_sems.at[d])
+            def fin_copy(k):
+                part = pl.ds(k * 8, 8)
+                return pltpu.make_async_copy(rest.at[part], fin_new.at[part], fin_sems.at[k])
 
             fluid_sweep(fluid, act, zlow, zhigh, 1, dims, lambda i: fluid_copy(i).start())
 
-            def layer(d, carry):
-                _, total = fin_neighbours(first, d, hlow, hhigh, fin_rows)
-                rest[d] = rest[d] + (OMEGA * FIN_CONDUCTION / DIAG) * total
-                fin_copy(d).start()
+            def layers(k, carry):
+                for j in range(8):
+                    d = k * 8 + j
+                    _, total = fin_neighbours(first, d, hlow, hhigh, fin_rows)
+                    rest[d] = rest[d] + (OMEGA * FIN_CONDUCTION / DIAG) * total
+                fin_copy(k).start()
                 return carry
 
-            lax.fori_loop(0, depth, layer, 0)
+            lax.fori_loop(0, depth // 8, layers, 0)
 
             def finish_fluid(i, carry):
                 fluid_copy(i).wait()
@@ -390,7 +408,7 @@
                 return carry
 
             lax.fori_loop(0, cells, finish_fluid, 0)
-            lax.fori_loop(0, depth, finish_fin, 0)
+            lax.fori_loop(0, depth // 8, finish_fin, 0)
 
         results = pl.pallas_call(
             end_kernel,
@@ -399,7 +417,7 @@
             in_specs=[vmem] * 10,
             out_specs=(vmem, vmem, vmem, hbm, hbm),
             scratch_shapes=scratch + [pltpu.SemaphoreType.DMA((cells,)),
-                                      pltpu.SemaphoreType.DMA((depth,))],
+                                      pltpu.SemaphoreType.DMA((depth // 8,))],
             input_output_aliases={0: 0, 1: 1, 2: 2},
             compiler_params=params,
             name="end",

time: 76.6 us -> 50.3 us (0.66)
  Pallas kernels: 42 us -> 15.8 us
    pallas_call x1, Pallas kernels: 19.9 us -> 6.97 us  [local(): pl.pallas_call(middle_kernel, out_shape=(fluid_pad, fin_pad, fin_pad, f32...]
    pallas_call x1, Pallas kernels: 10.8 us -> 2.21 us  [local(): pl.pallas_call(start_kernel, out_shape=(fluid_pad, fin_pad, f32(gx_rows,...]
    pallas_call x1, Pallas kernels: 11.4 us -> 6.59 us  [local(): pl.pallas_call(end_kernel, out_shape=(fluid_pad, fin_pad, f32(depth, fin_...]
where the time goes in v2:
time: 50.3 us; the launch traced here: 50 us
  starting transfers between devices  22.1 us (44%)
  Pallas kernels  15.8 us (31%)
  waiting for transfers between devices  7.19 us (14%)
  local copies, waits for them, and re-layouts  4.23 us (8%)
  between operations  0.74 us (1%)
    pallas_call x1, Pallas kernels, local(): pl.pallas_call(middle_kernel, out_shape=(fluid_pad, fin_pad, fin_pad, f32...  6.97 us
    ppermute x2, starting transfers between devices, local(): below = lax.ppermute(grpf, 'grp', chain(groups, 1))  6.96 us
    pallas_call x1, Pallas kernels, local(): pl.pallas_call(end_kernel, out_shape=(fluid_pad, fin_pad, f32(depth, fin_...  6.59 us
    ppermute x2, waiting for transfers between devices, local(): above = lax.ppermute(grpb, 'grp', chain(groups, -1))  6.45 us
    ppermute x2, starting transfers between devices, local(): above = lax.ppermute(grpb, 'grp', chain(groups, -1))  4.71 us
    ppermute x1, starting transfers between devices, local(): nxt = lax.ppermute(gxb, 'gx', chain(count, -1))  4.24 us
    unnamed x11, local copies, waits for them, and re-layouts  4.23 us
    ppermute x1, starting transfers between devices, local(): prev = lax.ppermute(gxf, 'gx', chain(count, 1))  2.5 us
  transfers between devices with their start and end apart: 11, of which 3 were waited for; matrix products, arithmetic and copies ran while one was open for 0% of the time, Pallas kernels for 0%

profile of v2, /device:TPU:12, one launch (start us, length us, event | category | flops | bytes accessed | tf_op | source)
XLA Modules:
  0.0 50.0 jit_solution(8732815894951294030)
XLA Ops:
  0.6 0.0 copy-start.1
  0.6 0.0 copy-start.2
  0.6 1.7 %copy.21.refs_3_ = f32[64,32,256]{2,1,0:T(8,128)S(1)} copy(f32[64,32,256]{2,1,0:T(8,128)} %param.9) | data formatting | bytes 4194304
  2.4 0.5 copy-done.1
  2.9 0.6 %copy-done.2 = f32[64,32,256]{2,1,0:T(8,128)S(1)} copy-done((f32[64,32,256]{2,1,0:T(8,128)S(1)}, f32[64,32,256]{2,1,0:T(8,128)}, u32[]{:S(2)}) %copy-start.2) | copy-done | bytes 2097176
  3.5 0.0 copy-start.3
  3.5 0.7 %copy-done.3 = s32[1,1,2048,1]{2,3,1,0:T(1,128)S(1)} copy-done((s32[1,1,2048,1]{2,3,1,0:T(1,128)S(1)}, s32[1,1,2048,1]{2,3,1,0:T(1,128)}, u32[]{:S(2)}) %copy-start.3) | copy-done | bytes 8216
  4.2 0.0 copy-start.4
  4.2 0.7 %copy-done.4 = s32[1,1,2048]{2,1,0:T(1,128)S(1)} copy-done((s32[1,1,2048]{2,1,0:T(1,128)S(1)}, s32[1,1,2048]{2,1,0:T(1,128)}, u32[]{:S(2)}) %copy-start.4) | copy-done | bytes 8216
  4.9 0.0 copy-start
  4.9 2.2 %start.1 = (f32[18,144,256]{2,1,0:T(8,128)S(1)}, f32[66,48,256]{2,1,0:T(8,128)S(1)}, f32[176,256]{1,0:T(8,128)S(1)}, f32[176,256]{1,0:T(8,128)S(1)}, f32[48,256]...) custom-call(f32[16,128,256]{2,1,0:T(8,128)S(1)} %copy-done.1, ...), custom_call_target="tpu_custom_call" | custom-call | tf_op jit(solution)/shard_map/start/pallas_call | solution.py:259
  7.1 1.5 %collective-permute-start = (f32[176,256]{1,0:T(8,128)S(1)}, f32[176,256]{1,0:T(8,128)S(1)}, u32[]{:S(2)}, u32[]{:S(2)}) collective-permute-start(f32[176,256]{1,0:T(8,128)S(1)} %get-tuple-element.23), channel_id=1, source_target_pairs={{0,2},{2,4},{4,6},{6,0},{1,3},{3,5},{5,7},{7,1},{8,10},{10,12},{12... | collective-permute-start | bytes 540680 | tf_op jit(solution)/shard_map/ppermute | solution.py:278
  8.6 1.4 %collective-permute-start.1 = (f32[176,256]{1,0:T(8,128)S(1)}, f32[176,256]{1,0:T(8,128)S(1)}, u32[]{:S(2)}, u32[]{:S(2)}) collective-permute-start(f32[176,256]{1,0:T(8,128)S(1)} %get-tuple-element.24), channel_id=1, source_target_pairs={{0,6},{2,0},{4,2},{6,4},{1,7},{3,1},{5,3},{7,5},{8,14},{10,8},{12,... | collective-permute-start | bytes 540680 | tf_op jit(solution)/shard_map/ppermute | solution.py:279
  10.1 3.5 %collective-permute-start.2 = (f32[48,256]{1,0:T(8,128)S(1)}, f32[48,256]{1,0:T(8,128)S(1)}, u32[]{:S(2)}, u32[]{:S(2)}) collective-permute-start(f32[48,256]{1,0:T(8,128)S(1)} %get-tuple-element.25), channel_id=1, source_target_pairs={{0,8},{8,16},{16,24},{1,9},{9,17},{17,25},{2,10},{10,18},{18,26},{... | collective-permute-start | bytes 147464 | tf_op jit(solution)/shard_map/ppermute | solution.py:285
  13.6 2.4 %collective-permute-start.3 = (f32[48,256]{1,0:T(8,128)S(1)}, f32[48,256]{1,0:T(8,128)S(1)}, u32[]{:S(2)}, u32[]{:S(2)}) collective-permute-start(f32[48,256]{1,0:T(8,128)S(1)} %get-tuple-element.26), channel_id=1, source_target_pairs={{8,0},{16,8},{24,16},{9,1},{17,9},{25,17},{10,2},{18,10},{26,18},{... | collective-permute-start | bytes 147464 | tf_op jit(solution)/shard_map/ppermute | solution.py:286
  15.9 0.1 collective-permute-start.4
  16.0 0.0 collective-permute-done.2.refs_6_
  16.0 0.5 %collective-permute-start.5 = (f32[48,256]{1,0:T(8,128)S(1)}, f32[48,256]{1,0:T(8,128)S(1)}, u32[]{:S(2)}, u32[]{:S(2)}) collective-permute-start(f32[48,256]{1,0:T(8,128)S(1)} %get-tuple-element.28.refs_9_), channel_id=1, source_target_pairs={{0,4},{2,6},{4,0},{6,2},{1,5},{3,7},{5,1},{7,3},{8,12},{10,14},{12... | collective-permute-start | bytes 147464 | tf_op jit(solution)/shard_map/ppermute | solution.py:280
  16.6 3.0 %collective-permute-done.3.refs_7_ = f32[48,256]{1,0:T(8,128)S(1)} collective-permute-done((f32[48,256]{1,0:T(8,128)S(1)}, f32[48,256]{1,0:T(8,128)S(1)}, u32[]{:S(2)}, u32[]{:S(2)}) %collective-permute-start.3) | collective-permute-done | bytes 49184 | tf_op jit(solution)/shard_map/ppermute | solution.py:286
  19.5 0.0 collective-permute-done.4.refs_8_
  19.5 0.6 %collective-permute-done.5.refs_10_ = f32[48,256]{1,0:T(8,128)S(1)} collective-permute-done((f32[48,256]{1,0:T(8,128)S(1)}, f32[48,256]{1,0:T(8,128)S(1)}, u32[]{:S(2)}, u32[]{:S(2)}) %collective-permute-start.5) | collective-permute-done | bytes 49184 | tf_op jit(solution)/shard_map/ppermute | solution.py:280
  20.2 0.0 collective-permute-done.refs_4_
  20.2 0.0 collective-permute-done.1.refs_5_
  20.2 0.0 copy-done
  20.2 7.0 %middle.1 = (f32[18,144,256]{2,1,0:T(8,128)S(1)}, f32[66,48,256]{2,1,0:T(8,128)S(1)}, f32[66,48,256]{2,1,0:T(8,128)S(1)}, f32[64,32,256]{2,1,0:T(8,128)S(1)}, f3...) custom-call(f32[18,144,256]{2,1,0:T(8,128)S(1)} %get-tuple-element.2, ...), custom_call_target="tpu_custom_call", output_to_operand_aliasing={{0}: (0, {}), {1}: (1, {}), {3}: (3, {})} | custom-call | tf_op jit(solution)/shard_map/middle/pallas_call | solution.py:353
  27.1 2.5 %collective-permute-start.6 = (f32[128,256]{1,0:T(8,128)S(1)}, f32[128,256]{1,0:T(8,128)S(1)}, u32[]{:S(2)}, u32[]{:S(2)}) collective-permute-start(f32[128,256]{1,0:T(8,128)S(1)} %get-tuple-element.33), channel_id=1, source_target_pairs={{0,2},{2,4},{4,6},{1,3},{3,5},{5,7},{8,10},{10,12},{12,14},{9,11},... | collective-permute-start | bytes 393224 | tf_op jit(solution)/shard_map/ppermute | solution.py:366
  29.7 4.2 %collective-permute-start.7 = (f32[128,256]{1,0:T(8,128)S(1)}, f32[128,256]{1,0:T(8,128)S(1)}, u32[]{:S(2)}, u32[]{:S(2)}) collective-permute-start(f32[128,256]{1,0:T(8,128)S(1)} %get-tuple-element.34), channel_id=1, source_target_pairs={{2,0},{4,2},{6,4},{3,1},{5,3},{7,5},{10,8},{12,10},{14,12},{11,9},... | collective-permute-start | bytes 393224 | tf_op jit(solution)/shard_map/ppermute | solution.py:367
  33.9 3.5 %collective-permute-start.8 = (f32[48,256]{1,0:T(8,128)S(1)}, f32[48,256]{1,0:T(8,128)S(1)}, u32[]{:S(2)}, u32[]{:S(2)}) collective-permute-start(f32[48,256]{1,0:T(8,128)S(1)} %get-tuple-element.35), channel_id=1, source_target_pairs={{0,8},{8,16},{16,24},{1,9},{9,17},{17,25},{2,10},{10,18},{18,26},{... | collective-permute-start | bytes 147464 | tf_op jit(solution)/shard_map/ppermute | solution.py:368
  37.4 2.4 %collective-permute-start.9 = (f32[48,256]{1,0:T(8,128)S(1)}, f32[48,256]{1,0:T(8,128)S(1)}, u32[]{:S(2)}, u32[]{:S(2)}) collective-permute-start(f32[48,256]{1,0:T(8,128)S(1)} %get-tuple-element.36), channel_id=1, source_target_pairs={{8,0},{16,8},{24,16},{9,1},{17,9},{25,17},{10,2},{18,10},{26,18},{... | collective-permute-start | bytes 147464 | tf_op jit(solution)/shard_map/ppermute | solution.py:369
  39.8 0.1 collective-permute-start.10
  39.8 0.0 collective-permute-done.8.below
  39.9 3.5 %collective-permute-done.9.above = f32[48,256]{1,0:T(8,128)S(1)} collective-permute-done((f32[48,256]{1,0:T(8,128)S(1)}, f32[48,256]{1,0:T(8,128)S(1)}, u32[]{:S(2)}, u32[]{:S(2)}) %collective-permute-start.9) | collective-permute-done | bytes 49184 | tf_op jit(solution)/shard_map/ppermute | solution.py:369
  43.4 0.0 collective-permute-done.10.side
  43.4 0.0 collective-permute-done.6.prev
  43.4 0.0 collective-permute-done.7.nxt
  43.4 6.6 %end.1 = (f32[18,144,256]{2,1,0:T(8,128)S(1)}, f32[66,48,256]{2,1,0:T(8,128)S(1)}, f32[64,32,256]{2,1,0:T(8,128)S(1)}, f32[16,128,256]{2,1,0:T(8,128)}, f32[64,32,256]{2,1,0:T(8,128)}) custom-call(f32[18,144,256]{2,1,0:T(8,128)S(1)} %get-tuple-element.29._0, ...), custom_call_target="tpu_custom_call", output_to_operand_aliasing={{0}: (0, {}), {1}: (1, {}), {2}: (2, {})} | custom-call | tf_op jit(solution)/shard_map/end/pallas_call | solution.py:413
Async XLA Ops:
  0.6 2.2 %copy-start.1 = (f32[16,128,256]{2,1,0:T(8,128)S(1)}, f32[16,128,256]{2,1,0:T(8,128)}, u32[]{:S(2)}) copy-start(f32[16,128,256]{2,1,0:T(8,128)} %fluid_hbm.1) | copy-start | bytes 6291460
  0.6 2.8 %copy-start.2 = (f32[64,32,256]{2,1,0:T(8,128)S(1)}, f32[64,32,256]{2,1,0:T(8,128)}, u32[]{:S(2)}) copy-start(f32[64,32,256]{2,1,0:T(8,128)} %fin_hbm.1) | copy-start | bytes 6291460
  3.5 0.7 %copy-start.3 = (s32[1,1,2048,1]{2,3,1,0:T(1,128)S(1)}, s32[1,1,2048,1]{2,3,1,0:T(1,128)}, u32[]{:S(2)}) copy-start(s32[1,1,2048,1]{2,3,1,0:T(1,128)} %param.10) | copy-start | bytes 24580
  4.2 0.7 %copy-start.4 = (s32[1,1,2048]{2,1,0:T(1,128)S(1)}, s32[1,1,2048]{2,1,0:T(1,128)}, u32[]{:S(2)}) copy-start(s32[1,1,2048]{2,1,0:T(1,128)} %param.11) | copy-start | bytes 24580
  4.9 15.3 %copy-start = (s32[16,128,256]{2,1,0:T(8,128)S(1)}, s32[16,128,256]{2,1,0:T(8,128)}, u32[]{:S(2)}) copy-start(s32[16,128,256]{2,1,0:T(8,128)} %act.1) | copy-start | bytes 6291460
  7.1 13.1 %collective-permute-start = (f32[176,256]{1,0:T(8,128)S(1)}, f32[176,256]{1,0:T(8,128)S(1)}, u32[]{:S(2)}, u32[]{:S(2)}) collective-permute-start(f32[176,256]{1,0:T(8,128)S(1)} %get-tuple-element.23), channel_id=1, source_target_pairs={{0,2},{2,4},{4,6},{6,0},{1,3},{3,5},{5,7},{7,1},{8,10},{10,12},{12... | collective-permute-start | bytes 540680 | tf_op jit(solution)/shard_map/ppermute | solution.py:278
  8.6 11.5 %collective-permute-start.1 = (f32[176,256]{1,0:T(8,128)S(1)}, f32[176,256]{1,0:T(8,128)S(1)}, u32[]{:S(2)}, u32[]{:S(2)}) collective-permute-start(f32[176,256]{1,0:T(8,128)S(1)} %get-tuple-element.24), channel_id=1, source_target_pairs={{0,6},{2,0},{4,2},{6,4},{1,7},{3,1},{5,3},{7,5},{8,14},{10,8},{12,... | collective-permute-start | bytes 540680 | tf_op jit(solution)/shard_map/ppermute | solution.py:279
  10.1 6.0 %collective-permute-start.2 = (f32[48,256]{1,0:T(8,128)S(1)}, f32[48,256]{1,0:T(8,128)S(1)}, u32[]{:S(2)}, u32[]{:S(2)}) collective-permute-start(f32[48,256]{1,0:T(8,128)S(1)} %get-tuple-element.25), channel_id=1, source_target_pairs={{0,8},{8,16},{16,24},{1,9},{9,17},{17,25},{2,10},{10,18},{18,26},{... | collective-permute-start | bytes 147464 | tf_op jit(solution)/shard_map/ppermute | solution.py:285
  13.6 6.0 %collective-permute-start.3 = (f32[48,256]{1,0:T(8,128)S(1)}, f32[48,256]{1,0:T(8,128)S(1)}, u32[]{:S(2)}, u32[]{:S(2)}) collective-permute-start(f32[48,256]{1,0:T(8,128)S(1)} %get-tuple-element.26), channel_id=1, source_target_pairs={{8,0},{16,8},{24,16},{9,1},{17,9},{25,17},{10,2},{18,10},{26,18},{... | collective-permute-start | bytes 147464 | tf_op jit(solution)/shard_map/ppermute | solution.py:286
  15.9 3.6 %collective-permute-start.4 = (f32[48,256]{1,0:T(8,128)S(1)}, f32[48,256]{1,0:T(8,128)S(1)}, u32[]{:S(2)}, u32[]{:S(2)}) collective-permute-start(f32[48,256]{1,0:T(8,128)S(1)} %get-tuple-element.27), channel_id=1, source_target_pairs={{0,1},{1,0},{2,3},{3,2},{4,5},{5,4},{6,7},{7,6},{8,9},{9,8},{10,11... | collective-permute-start | bytes 147464 | tf_op jit(solution)/shard_map/ppermute | solution.py:287
  16.0 4.1 %collective-permute-start.5 = (f32[48,256]{1,0:T(8,128)S(1)}, f32[48,256]{1,0:T(8,128)S(1)}, u32[]{:S(2)}, u32[]{:S(2)}) collective-permute-start(f32[48,256]{1,0:T(8,128)S(1)} %get-tuple-element.28.refs_9_), channel_id=1, source_target_pairs={{0,4},{2,6},{4,0},{6,2},{1,5},{3,7},{5,1},{7,3},{8,12},{10,14},{12... | collective-permute-start | bytes 147464 | tf_op jit(solution)/shard_map/ppermute | solution.py:280
  27.1 16.2 %collective-permute-start.6 = (f32[128,256]{1,0:T(8,128)S(1)}, f32[128,256]{1,0:T(8,128)S(1)}, u32[]{:S(2)}, u32[]{:S(2)}) collective-permute-start(f32[128,256]{1,0:T(8,128)S(1)} %get-tuple-element.33), channel_id=1, source_target_pairs={{0,2},{2,4},{4,6},{1,3},{3,5},{5,7},{8,10},{10,12},{12,14},{9,11},... | collective-permute-start | bytes 393224 | tf_op jit(solution)/shard_map/ppermute | solution.py:366
  29.7 13.7 %collective-permute-start.7 = (f32[128,256]{1,0:T(8,128)S(1)}, f32[128,256]{1,0:T(8,128)S(1)}, u32[]{:S(2)}, u32[]{:S(2)}) collective-permute-start(f32[128,256]{1,0:T(8,128)S(1)} %get-tuple-element.34), channel_id=1, source_target_pairs={{2,0},{4,2},{6,4},{3,1},{5,3},{7,5},{10,8},{12,10},{14,12},{11,9},... | collective-permute-start | bytes 393224 | tf_op jit(solution)/shard_map/ppermute | solution.py:367
  33.9 6.0 %collective-permute-start.8 = (f32[48,256]{1,0:T(8,128)S(1)}, f32[48,256]{1,0:T(8,128)S(1)}, u32[]{:S(2)}, u32[]{:S(2)}) collective-permute-start(f32[48,256]{1,0:T(8,128)S(1)} %get-tuple-element.35), channel_id=1, source_target_pairs={{0,8},{8,16},{16,24},{1,9},{9,17},{17,25},{2,10},{10,18},{18,26},{... | collective-permute-start | bytes 147464 | tf_op jit(solution)/shard_map/ppermute | solution.py:368
  37.4 6.0 %collective-permute-start.9 = (f32[48,256]{1,0:T(8,128)S(1)}, f32[48,256]{1,0:T(8,128)S(1)}, u32[]{:S(2)}, u32[]{:S(2)}) collective-permute-start(f32[48,256]{1,0:T(8,128)S(1)} %get-tuple-element.36), channel_id=1, source_target_pairs={{8,0},{16,8},{24,16},{9,1},{17,9},{25,17},{10,2},{18,10},{26,18},{... | collective-permute-start | bytes 147464 | tf_op jit(solution)/shard_map/ppermute | solution.py:369
  39.8 3.6 %collective-permute-start.10 = (f32[48,256]{1,0:T(8,128)S(1)}, f32[48,256]{1,0:T(8,128)S(1)}, u32[]{:S(2)}, u32[]{:S(2)}) collective-permute-start(f32[48,256]{1,0:T(8,128)S(1)} %get-tuple-element.37), channel_id=1, source_target_pairs={{0,1},{1,0},{2,3},{3,2},{4,5},{5,4},{6,7},{7,6},{8,9},{9,8},{10,11... | collective-permute-start | bytes 147464 | tf_op jit(solution)/shard_map/ppermute | solution.py:370

commit v3 on v2

--- a/solution.py
+++ b/solution.py
@@ -118,9 +118,15 @@
 
 
 def unpack_halos(fluid, fin, zlow, zhigh, hlow, hhigh, prev, nxt, below, above, side,
-                 low_face, gy, prev_on, next_on, dims):
+                 low_face, place, sizes, dims):
     cells, rows, width, depth, fin_rows, fin_width = dims
     half = rows // 2
+    grp, gx, gy = place
+    groups, count = sizes
+    below_on = jnp.where(grp == 0, 0.0, 1.0)
+    above_on = jnp.where(grp == groups - 1, 0.0, 1.0)
+    prev_on = jnp.where(gx == 0, 0.0, 1.0)
+    next_on = jnp.where(gx == count - 1, 0.0, 1.0)
     for plane, ref, on in ((0, prev, prev_on), (cells + 1, nxt, next_on)):
         packed = ref[0:half, :] * on
         fluid[plane, PAD : PAD + half, :] = packed
@@ -133,9 +139,9 @@
         fluid[i + 1, PAD + rows : PAD + rows + 1, :] = line * high_on
     blank = jnp.zeros((LANES - cells, rows), jnp.float32)
     zlow[...] = jnp.concatenate([low_face, blank], axis=0).T
-    zhigh[...] = jnp.concatenate([above[0:cells, 0:LANES], blank], axis=0).T
-    fin[0, PAD : PAD + fin_rows, :] = below[cells : cells + fin_rows, :]
-    fin[depth + 1, PAD : PAD + fin_rows, :] = above[cells : cells + fin_rows, :]
+    zhigh[...] = jnp.concatenate([above[0:cells, 0:LANES] * above_on, blank], axis=0).T
+    fin[0, PAD : PAD + fin_rows, :] = below[cells : cells + fin_rows, :] * below_on
+    fin[depth + 1, PAD : PAD + fin_rows, :] = above[cells : cells + fin_rows, :] * above_on
     columns = side[cells : cells + fin_rows, 0:LANES]
     hlow[...] = columns * low_on
     hhigh[...] = columns * high_on
@@ -214,6 +220,7 @@
         assert rows == LANES and width == fin_width == 2 * rows and fin_rows == 2 * cells
         assert depth <= LANES and depth % 8 == 0 and cells % 2 == 0 and rows % ROWS == 0 and fin_rows == ROWS
         dims = (cells, rows, width, depth, fin_rows, fin_width)
+        sizes = (groups, count)
         half = rows // 2
         face_rows = half + depth
         wall_rows = fin_rows + cells
@@ -227,9 +234,11 @@
         fin_pad = f32(depth + 2, fin_rows + 2 * PAD, fin_width)
         faces = (f32(small_rows, width), f32(small_rows, width), f32(small_rows, width))
 
-        def start_kernel(fluid_hbm, fin_hbm, own, tgt, fluid, fin, gxf, gxb, grpf, grpb, gyx,
-                         wall, sems):
+        def start_kernel(fluid_hbm, fin_hbm, own_hbm, tgt_hbm, fluid, fin, gxf, gxb, grpf, grpb,
+                         gyx, wall, own, tgt, sems):
             copies = (
+                pltpu.make_async_copy(own_hbm, own, sems.at[2]),
+                pltpu.make_async_copy(tgt_hbm, tgt, sems.at[3]),
                 pltpu.make_async_copy(
                     fluid_hbm, fluid.at[pl.ds(1, cells), pl.ds(PAD, rows), :], sems.at[0]
                 ),
@@ -241,12 +250,12 @@
                 copy.start()
             gy = lax.axis_index("gy")
             shape = (cells, rows)
+            for copy in copies:
+                copy.wait()
             shift = tgt[...] - 2 * (iota(shape, 0) * fin_width + iota(shape, 1))
             row_shift = (shift >= fin_width).astype(jnp.int32)
             code = own[...] * 4 + row_shift * 2 + (shift - row_shift * fin_width)
             wall[fin_rows:, LANES:] = code.astype(jnp.float32)
-            for copy in copies:
-                copy.wait()
             bottom = pack_faces(fluid, fin, 1, gxf, gxb, grpf, grpb, gyx, gy, dims)
             wall[fin_rows:, 0:LANES] = bottom
             surface = fin[1, PAD : PAD + fin_rows, :]
@@ -260,40 +269,37 @@
             start_kernel,
             out_shape=(fluid_pad, fin_pad, f32(gx_rows, width), f32(gx_rows, width)) + faces
             + (f32(wall_rows, width),),
-            in_specs=[hbm, hbm, vmem, vmem],
+            in_specs=[pl.BlockSpec(memory_space=pltpu.HBM)] * 4,
             out_specs=(vmem,) * 8,
-            scratch_shapes=[pltpu.SemaphoreType.DMA((2,))],
+            scratch_shapes=[pltpu.VMEM((cells, rows), jnp.int32), pltpu.VMEM((cells, rows), jnp.int32),
+                            pltpu.SemaphoreType.DMA((4,))],
             compiler_params=params,
             name="start",
-        )(fluid_temp, fin_temp, owners, targets)
-
-        def chain(size, step):
-            return [(i, i + step) for i in range(size) if 0 <= i + step < size]
+        )(*(pltpu.with_memory_space_constraint(v, pltpu.HBM)
+            for v in (fluid_temp, fin_temp, owners, targets)))
 
         def around(size, step):
             return [(i, (i + step) % size) for i in range(size)]
 
         swap = [(0, 1), (1, 0)]
+        prev = lax.ppermute(gxf, "gx", around(count, 1))
+        nxt = lax.ppermute(gxb, "gx", around(count, -1))
         if ring:
-            prev = lax.ppermute(gxf, "gx", around(count, 1))
-            nxt = lax.ppermute(gxb, "gx", around(count, -1))
             walls = [wall] + [lax.ppermute(wall, "gx", around(count, k)) for k in range(2, count - 1)]
         else:
-            prev = lax.ppermute(gxf, "gx", chain(count, 1))
-            nxt = lax.ppermute(gxb, "gx", chain(count, -1))
             walls = [wall, lax.all_gather(wall, "gx")]
-        below = lax.ppermute(grpf, "grp", chain(groups, 1))
-        above = lax.ppermute(grpb, "grp", chain(groups, -1))
+        below = lax.ppermute(grpf, "grp", around(groups, 1))
+        above = lax.ppermute(grpb, "grp", around(groups, -1))
         side = lax.ppermute(gyx, "gy", swap)
 
         def middle_kernel(*refs):
-            (act, prev, nxt, below, above, side), refs = (refs[2],) + refs[4:9], refs[9:]
+            (act, src, prev, nxt, below, above, side), refs = refs[2:9], refs[9:]
             wall_refs, refs = refs[: len(walls)], refs[len(walls) :]
-            fluid, fin, first, src, ghost_out, gxf, gxb, grpf, grpb, gyx = refs[:10]
-            zlow, zhigh, hlow, hhigh = refs[10:]
-            gx = lax.axis_index("gx")
-            gy = lax.axis_index("gy")
-            on_wall = lax.axis_index("grp") == 0
+            fluid, fin, first, rest, ghost_out, gxf, gxb, grpf, grpb, gyx = refs[:10]
+            zlow, zhigh, hlow, hhigh, deposit = refs[10:]
+            place = [lax.axis_index(name) for name in ("grp", "gx", "gy")]
+            grp, gx, gy = place
+            on_wall = grp == 0
             own = wall_refs[0]
             own_code = own[fin_rows:, LANES:]
             if ring:
@@ -325,22 +331,26 @@
                     axis=0,
                 )
                 mixed = dot(split, interleave_matrix(fin_width), ((1,), (1,)))
-                src[0] = src[0] + dot(interleave_matrix(fin_rows), mixed, ((1,), (0,)))
+                deposit[...] = dot(interleave_matrix(fin_rows), mixed, ((1,), (0,)))
+
+            @pl.when(jnp.logical_not(on_wall))
+            def _():
+                deposit[...] = jnp.zeros((fin_rows, fin_width), jnp.float32)
 
             low_face = jnp.where(on_wall, ghost, below[0:cells, 0:LANES])
-            prev_on = jnp.where(gx == 0, 0.0, 1.0)
-            next_on = jnp.where(gx == count - 1, 0.0, 1.0)
             unpack_halos(fluid, fin, zlow, zhigh, hlow, hhigh, prev, nxt, below, above, side,
-                         low_face, gy, prev_on, next_on, dims)
+                         low_face, place, sizes, dims)
             fluid_sweep(fluid, act, zlow, zhigh, 0, dims)
 
             def layer(d):
                 here, total = fin_neighbours(fin, d, hlow, hhigh, fin_rows)
                 rhs = here + src[d]
                 first[d + 1, PAD : PAD + fin_rows, :] = (rhs + FIN_CONDUCTION * total) * (1.0 / DIAG)
-                src[d] = rhs * (OMEGA / DIAG) + here * (1.0 - OMEGA)
+                rest[d] = rhs * (OMEGA / DIAG) + here * (1.0 - OMEGA)
 
             repeat(depth, layer)
+            first[1, PAD : PAD + fin_rows, :] += deposit[...] * (1.0 / DIAG)
+            rest[0] += deposit[...] * (OMEGA / DIAG)
             pack_faces(fluid, first, 0, gxf, gxb, grpf, grpb, gyx, gy, dims)
 
         received = (prev, nxt, below, above, side)
@@ -356,27 +366,27 @@
                        f32(cells, rows), f32(face_rows, width), f32(face_rows, width)) + faces,
             in_specs=[vmem] * (9 + len(walls)),
             out_specs=(vmem,) * 10,
-            scratch_shapes=scratch,
-            input_output_aliases={0: 0, 1: 1, 3: 3},
+            scratch_shapes=scratch + [pltpu.VMEM((fin_rows, fin_width), jnp.float32)],
+            input_output_aliases={0: 0, 1: 1},
             compiler_params=params,
             name="middle",
         )(fluid0, fin0, active, fin_source, *received, *walls)
         fluid1, _, first, rest, ghost, gxf, gxb, grpf, grpb, gyx = outs
 
-        prev = lax.ppermute(gxf, "gx", chain(count, 1))
-        nxt = lax.ppermute(gxb, "gx", chain(count, -1))
-        below = lax.ppermute(grpf, "grp", chain(groups, 1))
-        above = lax.ppermute(grpb, "grp", chain(groups, -1))
+        prev = lax.ppermute(gxf, "gx", around(count, 1))
+        nxt = lax.ppermute(gxb, "gx", around(count, -1))
+        below = lax.ppermute(grpf, "grp", around(groups, 1))
+        above = lax.ppermute(grpb, "grp", around(groups, -1))
         side = lax.ppermute(gyx, "gy", swap)
 
         def end_kernel(_0, _1, _2, act, ghost, prev, nxt, below, above, side,
                        fluid, first, rest, fluid_new, fin_new,
                        zlow, zhigh, hlow, hhigh, fluid_sems, fin_sems):
-            gy = lax.axis_index("gy")
-            on_wall = lax.axis_index("grp") == 0
+            place = [lax.axis_index(name) for name in ("grp", "gx", "gy")]
+            on_wall = place[0] == 0
             low_face = jnp.where(on_wall, ghost[...], below[0:cells, 0:LANES])
             unpack_halos(fluid, first, zlow, zhigh, hlow, hhigh, prev, nxt, below, above, side,
-                         low_face, gy, 1.0, 1.0, dims)
+                         low_face, place, sizes, dims)
 
             def fluid_copy(i):
                 return pltpu.make_async_copy(

time: 50.3 us -> 42.6 us (0.85)
  the two profiles are of different devices: /device:TPU:12 before, /device:TPU:0 now
where the time goes in v3:
time: 42.6 us; the launch traced here: 42.5 us
  Pallas kernels  18.2 us (43%)
  starting transfers between devices  16.5 us (39%)
  waiting for transfers between devices  7.07 us (17%)
  between operations  0.7 us (2%)
    pallas_call x1, Pallas kernels, local(): pl.pallas_call(middle_kernel, out_shape=(fluid_pad, fin_pad, fin_pad, f32...  7.43 us
    pallas_call x1, Pallas kernels, local(): pl.pallas_call(end_kernel, out_shape=(fluid_pad, fin_pad, f32(depth, fin_...  6.6 us
    ppermute x2, starting transfers between devices, local(): above = lax.ppermute(grpb, 'grp', around(groups, -1))  5.85 us
    ppermute x2, waiting for transfers between devices, local(): below = lax.ppermute(grpf, 'grp', around(groups, 1))  4.6 us
    pallas_call x1, Pallas kernels, local(): pl.pallas_call(start_kernel, out_shape=(fluid_pad, fin_pad, f32(gx_rows,...  4.2 us
    ppermute x2, starting transfers between devices, local(): prev = lax.ppermute(gxf, 'gx', around(count, 1))  3.77 us
    ppermute x2, starting transfers between devices, local(): nxt = lax.ppermute(gxb, 'gx', around(count, -1))  3.25 us
    ppermute x1, waiting for transfers between devices, local(): lax.ppermute(wall, 'gx', around(count, k))  2.46 us
  transfers between devices with their start and end apart: 11, of which 3 were waited for; matrix products, arithmetic and copies ran while one was open for 0% of the time, Pallas kernels for 0%

profile of v3, /device:TPU:0, one launch (start us, length us, event | category | flops | bytes accessed | tf_op | source)
XLA Modules:
  0.0 42.5 jit_solution(8230140910364560361)
XLA Ops:
  0.6 0.0 copy-start
  0.6 0.0 copy-start.1
  0.7 4.2 %start.1 = (f32[18,144,256]{2,1,0:T(8,128)S(1)}, f32[66,48,256]{2,1,0:T(8,128)S(1)}, f32[176,256]{1,0:T(8,128)S(1)}, f32[176,256]{1,0:T(8,128)S(1)}, f32[48,256]...) custom-call(f32[16,128,256]{2,1,0:T(8,128)} %fluid_hbm.1, ...), custom_call_target="tpu_custom_call" | custom-call | tf_op jit(solution)/shard_map/start/pallas_call | solution.py:268
  4.9 3.0 %collective-permute-start = (f32[176,256]{1,0:T(8,128)S(1)}, f32[176,256]{1,0:T(8,128)S(1)}, u32[]{:S(2)}, u32[]{:S(2)}) collective-permute-start(f32[176,256]{1,0:T(8,128)S(1)} %get-tuple-element.23), channel_id=1, source_target_pairs={{0,2},{2,4},{4,6},{6,0},{1,3},{3,5},{5,7},{7,1},{8,10},{10,12},{12... | collective-permute-start | bytes 540680 | tf_op jit(solution)/shard_map/ppermute | solution.py:285
  7.9 1.0 %collective-permute-start.1 = (f32[176,256]{1,0:T(8,128)S(1)}, f32[176,256]{1,0:T(8,128)S(1)}, u32[]{:S(2)}, u32[]{:S(2)}) collective-permute-start(f32[176,256]{1,0:T(8,128)S(1)} %get-tuple-element.24), channel_id=1, source_target_pairs={{0,6},{2,0},{4,2},{6,4},{1,7},{3,1},{5,3},{7,5},{8,14},{10,8},{12,... | collective-permute-start | bytes 540680 | tf_op jit(solution)/shard_map/ppermute | solution.py:286
  8.9 2.0 %collective-permute-start.2 = (f32[48,256]{1,0:T(8,128)S(1)}, f32[48,256]{1,0:T(8,128)S(1)}, u32[]{:S(2)}, u32[]{:S(2)}) collective-permute-start(f32[48,256]{1,0:T(8,128)S(1)} %get-tuple-element.25), channel_id=1, source_target_pairs={{0,8},{8,16},{16,24},{24,0},{1,9},{9,17},{17,25},{25,1},{2,10},{10... | collective-permute-start | bytes 147464 | tf_op jit(solution)/shard_map/ppermute | solution.py:291
  10.9 2.0 %collective-permute-start.3 = (f32[48,256]{1,0:T(8,128)S(1)}, f32[48,256]{1,0:T(8,128)S(1)}, u32[]{:S(2)}, u32[]{:S(2)}) collective-permute-start(f32[48,256]{1,0:T(8,128)S(1)} %get-tuple-element.26), channel_id=1, source_target_pairs={{0,24},{8,0},{16,8},{24,16},{1,25},{9,1},{17,9},{25,17},{2,26},{10... | collective-permute-start | bytes 147464 | tf_op jit(solution)/shard_map/ppermute | solution.py:292
  12.9 0.0 collective-permute-start.4
  12.9 2.5 %collective-permute-done.2.refs_6_ = f32[48,256]{1,0:T(8,128)S(1)} collective-permute-done((f32[48,256]{1,0:T(8,128)S(1)}, f32[48,256]{1,0:T(8,128)S(1)}, u32[]{:S(2)}, u32[]{:S(2)}) %collective-permute-start.2) | collective-permute-done | bytes 49184 | tf_op jit(solution)/shard_map/ppermute | solution.py:291
  15.5 1.6 %collective-permute-start.5 = (f32[48,256]{1,0:T(8,128)S(1)}, f32[48,256]{1,0:T(8,128)S(1)}, u32[]{:S(2)}, u32[]{:S(2)}) collective-permute-start(f32[48,256]{1,0:T(8,128)S(1)} %get-tuple-element.28.refs_9_), channel_id=1, source_target_pairs={{0,4},{2,6},{4,0},{6,2},{1,5},{3,7},{5,1},{7,3},{8,12},{10,14},{12... | collective-permute-start | bytes 147464 | tf_op jit(solution)/shard_map/ppermute | solution.py:288
  17.1 0.0 collective-permute-done.3.refs_7_
  17.1 0.0 collective-permute-done.4.refs_8_
  17.1 2.5 %collective-permute-done.5.refs_10_ = f32[48,256]{1,0:T(8,128)S(1)} collective-permute-done((f32[48,256]{1,0:T(8,128)S(1)}, f32[48,256]{1,0:T(8,128)S(1)}, u32[]{:S(2)}, u32[]{:S(2)}) %collective-permute-start.5) | collective-permute-done | bytes 49184 | tf_op jit(solution)/shard_map/ppermute | solution.py:288
  19.5 0.0 collective-permute-done.refs_4_
  19.5 0.0 collective-permute-done.1.refs_5_
  19.6 0.0 copy-done
  19.6 0.0 copy-done.1
  19.6 7.4 %middle.1 = (f32[18,144,256]{2,1,0:T(8,128)S(1)}, f32[66,48,256]{2,1,0:T(8,128)S(1)}, f32[66,48,256]{2,1,0:T(8,128)S(1)}, f32[64,32,256]{2,1,0:T(8,128)S(1)}, f3...) custom-call(f32[18,144,256]{2,1,0:T(8,128)S(1)} %get-tuple-element.2, ...), custom_call_target="tpu_custom_call", output_to_operand_aliasing={{0}: (0, {}), {1}: (1, {})} | custom-call | tf_op jit(solution)/shard_map/middle/pallas_call | solution.py:363
  27.0 0.8 %collective-permute-start.6 = (f32[128,256]{1,0:T(8,128)S(1)}, f32[128,256]{1,0:T(8,128)S(1)}, u32[]{:S(2)}, u32[]{:S(2)}) collective-permute-start(f32[128,256]{1,0:T(8,128)S(1)} %get-tuple-element.33), channel_id=1, source_target_pairs={{0,2},{2,4},{4,6},{6,0},{1,3},{3,5},{5,7},{7,1},{8,10},{10,12},{12... | collective-permute-start | bytes 393224 | tf_op jit(solution)/shard_map/ppermute | solution.py:376
  27.8 2.2 %collective-permute-start.7 = (f32[128,256]{1,0:T(8,128)S(1)}, f32[128,256]{1,0:T(8,128)S(1)}, u32[]{:S(2)}, u32[]{:S(2)}) collective-permute-start(f32[128,256]{1,0:T(8,128)S(1)} %get-tuple-element.34), channel_id=1, source_target_pairs={{0,6},{2,0},{4,2},{6,4},{1,7},{3,1},{5,3},{7,5},{8,14},{10,8},{12,... | collective-permute-start | bytes 393224 | tf_op jit(solution)/shard_map/ppermute | solution.py:377
  30.0 0.0 collective-permute-start.8
  30.0 3.8 %collective-permute-start.9 = (f32[48,256]{1,0:T(8,128)S(1)}, f32[48,256]{1,0:T(8,128)S(1)}, u32[]{:S(2)}, u32[]{:S(2)}) collective-permute-start(f32[48,256]{1,0:T(8,128)S(1)} %get-tuple-element.36), channel_id=1, source_target_pairs={{0,24},{8,0},{16,8},{24,16},{1,25},{9,1},{17,9},{25,17},{2,26},{10... | collective-permute-start | bytes 147464 | tf_op jit(solution)/shard_map/ppermute | solution.py:379
  33.8 0.0 collective-permute-start.10
  33.8 2.1 %collective-permute-done.8.below = f32[48,256]{1,0:T(8,128)S(1)} collective-permute-done((f32[48,256]{1,0:T(8,128)S(1)}, f32[48,256]{1,0:T(8,128)S(1)}, u32[]{:S(2)}, u32[]{:S(2)}) %collective-permute-start.8) | collective-permute-done | bytes 49184 | tf_op jit(solution)/shard_map/ppermute | solution.py:378
  35.9 0.0 collective-permute-done.9.above
  35.9 0.0 collective-permute-done.10.side
  35.9 0.0 collective-permute-done.6.prev
  35.9 0.0 collective-permute-done.7.nxt
  35.9 6.6 %end.1 = (f32[18,144,256]{2,1,0:T(8,128)S(1)}, f32[66,48,256]{2,1,0:T(8,128)S(1)}, f32[64,32,256]{2,1,0:T(8,128)S(1)}, f32[16,128,256]{2,1,0:T(8,128)}, f32[64,32,256]{2,1,0:T(8,128)}) custom-call(f32[18,144,256]{2,1,0:T(8,128)S(1)} %get-tuple-element.29._0, ...), custom_call_target="tpu_custom_call", output_to_operand_aliasing={{0}: (0, {}), {1}: (1, {}), {2}: (2, {})} | custom-call | tf_op jit(solution)/shard_map/end/pallas_call | solution.py:423
Async XLA Ops:
  0.6 18.9 %copy-start = (s32[16,128,256]{2,1,0:T(8,128)S(1)}, s32[16,128,256]{2,1,0:T(8,128)}, u32[]{:S(2)}) copy-start(s32[16,128,256]{2,1,0:T(8,128)} %act.1) | copy-start | bytes 6291460
  0.6 18.9 %copy-start.1 = (f32[64,32,256]{2,1,0:T(8,128)S(1)}, f32[64,32,256]{2,1,0:T(8,128)}, u32[]{:S(2)}) copy-start(f32[64,32,256]{2,1,0:T(8,128)} %refs_3_.1) | copy-start | bytes 6291460
  4.9 14.7 %collective-permute-start = (f32[176,256]{1,0:T(8,128)S(1)}, f32[176,256]{1,0:T(8,128)S(1)}, u32[]{:S(2)}, u32[]{:S(2)}) collective-permute-start(f32[176,256]{1,0:T(8,128)S(1)} %get-tuple-element.23), channel_id=1, source_target_pairs={{0,2},{2,4},{4,6},{6,0},{1,3},{3,5},{5,7},{7,1},{8,10},{10,12},{12... | collective-permute-start | bytes 540680 | tf_op jit(solution)/shard_map/ppermute | solution.py:285
  7.9 11.7 %collective-permute-start.1 = (f32[176,256]{1,0:T(8,128)S(1)}, f32[176,256]{1,0:T(8,128)S(1)}, u32[]{:S(2)}, u32[]{:S(2)}) collective-permute-start(f32[176,256]{1,0:T(8,128)S(1)} %get-tuple-element.24), channel_id=1, source_target_pairs={{0,6},{2,0},{4,2},{6,4},{1,7},{3,1},{5,3},{7,5},{8,14},{10,8},{12,... | collective-permute-start | bytes 540680 | tf_op jit(solution)/shard_map/ppermute | solution.py:286
  8.9 6.6 %collective-permute-start.2 = (f32[48,256]{1,0:T(8,128)S(1)}, f32[48,256]{1,0:T(8,128)S(1)}, u32[]{:S(2)}, u32[]{:S(2)}) collective-permute-start(f32[48,256]{1,0:T(8,128)S(1)} %get-tuple-element.25), channel_id=1, source_target_pairs={{0,8},{8,16},{16,24},{24,0},{1,9},{9,17},{17,25},{25,1},{2,10},{10... | collective-permute-start | bytes 147464 | tf_op jit(solution)/shard_map/ppermute | solution.py:291
  10.9 6.2 %collective-permute-start.3 = (f32[48,256]{1,0:T(8,128)S(1)}, f32[48,256]{1,0:T(8,128)S(1)}, u32[]{:S(2)}, u32[]{:S(2)}) collective-permute-start(f32[48,256]{1,0:T(8,128)S(1)} %get-tuple-element.26), channel_id=1, source_target_pairs={{0,24},{8,0},{16,8},{24,16},{1,25},{9,1},{17,9},{25,17},{2,26},{10... | collective-permute-start | bytes 147464 | tf_op jit(solution)/shard_map/ppermute | solution.py:292
  12.9 4.2 %collective-permute-start.4 = (f32[48,256]{1,0:T(8,128)S(1)}, f32[48,256]{1,0:T(8,128)S(1)}, u32[]{:S(2)}, u32[]{:S(2)}) collective-permute-start(f32[48,256]{1,0:T(8,128)S(1)} %get-tuple-element.27), channel_id=1, source_target_pairs={{0,1},{1,0},{2,3},{3,2},{4,5},{5,4},{6,7},{7,6},{8,9},{9,8},{10,11... | collective-permute-start | bytes 147464 | tf_op jit(solution)/shard_map/ppermute | solution.py:293
  15.5 4.1 %collective-permute-start.5 = (f32[48,256]{1,0:T(8,128)S(1)}, f32[48,256]{1,0:T(8,128)S(1)}, u32[]{:S(2)}, u32[]{:S(2)}) collective-permute-start(f32[48,256]{1,0:T(8,128)S(1)} %get-tuple-element.28.refs_9_), channel_id=1, source_target_pairs={{0,4},{2,6},{4,0},{6,2},{1,5},{3,7},{5,1},{7,3},{8,12},{10,14},{12... | collective-permute-start | bytes 147464 | tf_op jit(solution)/shard_map/ppermute | solution.py:288
  27.0 8.9 %collective-permute-start.6 = (f32[128,256]{1,0:T(8,128)S(1)}, f32[128,256]{1,0:T(8,128)S(1)}, u32[]{:S(2)}, u32[]{:S(2)}) collective-permute-start(f32[128,256]{1,0:T(8,128)S(1)} %get-tuple-element.33), channel_id=1, source_target_pairs={{0,2},{2,4},{4,6},{6,0},{1,3},{3,5},{5,7},{7,1},{8,10},{10,12},{12... | collective-permute-start | bytes 393224 | tf_op jit(solution)/shard_map/ppermute | solution.py:376
  27.8 8.1 %collective-permute-start.7 = (f32[128,256]{1,0:T(8,128)S(1)}, f32[128,256]{1,0:T(8,128)S(1)}, u32[]{:S(2)}, u32[]{:S(2)}) collective-permute-start(f32[128,256]{1,0:T(8,128)S(1)} %get-tuple-element.34), channel_id=1, source_target_pairs={{0,6},{2,0},{4,2},{6,4},{1,7},{3,1},{5,3},{7,5},{8,14},{10,8},{12,... | collective-permute-start | bytes 393224 | tf_op jit(solution)/shard_map/ppermute | solution.py:377
  30.0 5.9 %collective-permute-start.8 = (f32[48,256]{1,0:T(8,128)S(1)}, f32[48,256]{1,0:T(8,128)S(1)}, u32[]{:S(2)}, u32[]{:S(2)}) collective-permute-start(f32[48,256]{1,0:T(8,128)S(1)} %get-tuple-element.35), channel_id=1, source_target_pairs={{0,8},{8,16},{16,24},{24,0},{1,9},{9,17},{17,25},{25,1},{2,10},{10... | collective-permute-start | bytes 147464 | tf_op jit(solution)/shard_map/ppermute | solution.py:378
  30.0 5.9 %collective-permute-start.9 = (f32[48,256]{1,0:T(8,128)S(1)}, f32[48,256]{1,0:T(8,128)S(1)}, u32[]{:S(2)}, u32[]{:S(2)}) collective-permute-start(f32[48,256]{1,0:T(8,128)S(1)} %get-tuple-element.36), channel_id=1, source_target_pairs={{0,24},{8,0},{16,8},{24,16},{1,25},{9,1},{17,9},{25,17},{2,26},{10... | collective-permute-start | bytes 147464 | tf_op jit(solution)/shard_map/ppermute | solution.py:379
  33.8 2.1 %collective-permute-start.10 = (f32[48,256]{1,0:T(8,128)S(1)}, f32[48,256]{1,0:T(8,128)S(1)}, u32[]{:S(2)}, u32[]{:S(2)}) collective-permute-start(f32[48,256]{1,0:T(8,128)S(1)} %get-tuple-element.37), channel_id=1, source_target_pairs={{0,1},{1,0},{2,3},{3,2},{4,5},{5,4},{6,7},{7,6},{8,9},{9,8},{10,11... | collective-permute-start | bytes 147464 | tf_op jit(solution)/shard_map/ppermute | solution.py:380

commit v4 on v3

--- a/solution.py
+++ b/solution.py
@@ -95,19 +95,20 @@
         gyx[i : i + 1, :] = fluid[i + 1, pl.ds(edge, 1), :]
     lane = iota((fin_rows, LANES), 1)
 
-    def columns(at):
+    def columns(at, side):
         kept = jnp.zeros((fin_rows, LANES), jnp.float32)
         for d in range(depth):
-            kept = jnp.where(lane == d, fin[d + 1, PAD : PAD + fin_rows, at : at + 1], kept)
+            column = fin[d + 1, PAD : PAD + fin_rows, at : at + 1]
+            kept = jnp.where(lane == 2 * d + side, column, kept)
         gyx[cells : cells + fin_rows, 0:LANES] = kept
 
     @pl.when(gy == 0)
     def _():
-        columns(fin_width - 1)
+        columns(fin_width - 1, 1)
 
     @pl.when(gy != 0)
     def _():
-        columns(0)
+        columns(0, 0)
 
     def lines(d):
         gxf[pl.ds(half + d, 1), :] = fin[d + 1, PAD + fin_rows - 1 : PAD + fin_rows, :]
@@ -117,8 +118,8 @@
     return low
 
 
-def unpack_halos(fluid, fin, zlow, zhigh, hlow, hhigh, prev, nxt, below, above, side,
-                 low_face, place, sizes, dims):
+def unpack_halos(fluid, fin, zrows, zedge, prev, nxt, below, above, side, low_face, colour,
+                 place, sizes, dims):
     cells, rows, width, depth, fin_rows, fin_width = dims
     half = rows // 2
     grp, gx, gy = place
@@ -137,14 +138,16 @@
         line = side[i : i + 1, :]
         fluid[i + 1, PAD - 1 : PAD, :] = line * low_on
         fluid[i + 1, PAD + rows : PAD + rows + 1, :] = line * high_on
-    blank = jnp.zeros((LANES - cells, rows), jnp.float32)
-    zlow[...] = jnp.concatenate([low_face, blank], axis=0).T
-    zhigh[...] = jnp.concatenate([above[0:cells, 0:LANES] * above_on, blank], axis=0).T
+    high_face = above[0:cells, 0:LANES] * above_on
+    odd_row = (iota((1, rows), 1) & 1) == 1
+    for k in range(cells // 2):
+        for lane, face, swap in ((2 * k, high_face, colour == 1), (2 * k + 1, low_face, colour == 0)):
+            first, second = face[2 * k : 2 * k + 1, :], face[2 * k + 1 : 2 * k + 2, :]
+            zrows[lane : lane + 1, :] = jnp.where(odd_row == swap, second, first)
+    zrows[cells:, :] = jnp.zeros((LANES - cells, rows), jnp.float32)
+    zedge[...] = zrows[...].T
     fin[0, PAD : PAD + fin_rows, :] = below[cells : cells + fin_rows, :] * below_on
     fin[depth + 1, PAD : PAD + fin_rows, :] = above[cells : cells + fin_rows, :] * above_on
-    columns = side[cells : cells + fin_rows, 0:LANES]
-    hlow[...] = columns * low_on
-    hhigh[...] = columns * high_on
 
     def line_of(d):
         fin[d + 1, PAD - 1 : PAD, :] = prev[pl.ds(half + d, 1), :] * prev_on
@@ -153,45 +156,56 @@
     repeat(depth, line_of)
 
 
-def fluid_sweep(fluid, active, zlow, zhigh, colour, dims, done=None):
+def fluid_sweep(fluid, active, zedge, other, colour, dims, done=None):
     cells, rows, width, depth, fin_rows, fin_width = dims
     parity = (iota((ROWS, width), 0) + iota((ROWS, width), 1)) & 1
-
-    def plane(i, carry):
-        off = parity ^ ((i + colour) & 1)
+    updating = parity == colour
+    off = parity ^ colour
+    end_parity = iota((1, width), 1) & 1
+
+    def pair(k, carry):
+        a, b = 2 * k + 1, 2 * k + 2
+        for at, swap in ((PAD - 1, 1 - colour), (PAD + rows, colour)):
+            line = slice(at, at + 1)
+            other[line, :] = jnp.where(end_parity == swap, fluid[b, line, :], fluid[a, line, :])
         for start in range(0, rows, ROWS):
             inner = slice(PAD + start, PAD + start + ROWS)
-            here = fluid[i + 1, inner, :]
-            low = pltpu.roll(zlow[start : start + ROWS, :], (LANES - i) % LANES, axis=1)
-            high = pltpu.roll(zhigh[start : start + ROWS, :], LANES - 1 - i, axis=1)
-            total = (
-                fluid[i, inner, :]
-                + fluid[i + 2, inner, :]
-                + fluid[i + 1, PAD + start - 1 : PAD + start + ROWS - 1, :]
-                + fluid[i + 1, PAD + start + 1 : PAD + start + ROWS + 1, :]
-                + lane_neighbours(here, low, high)
+            other[inner, :] = jnp.where(updating, fluid[b, inner, :], fluid[a, inner, :])
+        for start in range(0, rows, ROWS):
+            inner = slice(PAD + start, PAD + start + ROWS)
+            edge = pltpu.roll(zedge[start : start + ROWS, :], LANES - 1 - 2 * k, axis=1)
+            shared = (
+                other[PAD + start - 1 : PAD + start + ROWS - 1, :]
+                + other[PAD + start + 1 : PAD + start + ROWS + 1, :]
+                + lane_neighbours(other[inner, :], edge, edge)
             )
-            updated = (here + FLUID_DIFFUSION * total) * FLUID_SCALE
-            mask = active[i, start : start + ROWS, :] > off
-            fluid[i + 1, inner, :] = jnp.where(mask, updated, here)
+            here_a = fluid[a, inner, :]
+            here_b = fluid[b, inner, :]
+            total_a = shared + fluid[a - 1, inner, :] + here_b
+            total_b = shared + fluid[b + 1, inner, :] + here_a
+            new_a = (here_a + FLUID_DIFFUSION * total_a) * FLUID_SCALE
+            new_b = (here_b + FLUID_DIFFUSION * total_b) * FLUID_SCALE
+            mask_a = active[a - 1, start : start + ROWS, :] > off
+            mask_b = active[b - 1, start : start + ROWS, :] > 1 - off
+            fluid[a, inner, :] = jnp.where(mask_a, new_a, here_a)
+            fluid[b, inner, :] = jnp.where(mask_b, new_b, here_b)
         if done is not None:
-            done(i)
+            done(k)
         return carry
 
-    lax.fori_loop(0, cells, plane, 0)
-
-
-def fin_neighbours(fin, d, hlow, hhigh, fin_rows):
+    lax.fori_loop(0, cells // 2, pair, 0)
+
+
+def fin_neighbours(fin, d, hedge, fin_rows):
     inner = slice(PAD, PAD + fin_rows)
     here = fin[d + 1, inner, :]
-    low = pltpu.roll(hlow[...], (LANES - d) % LANES, axis=1)
-    high = pltpu.roll(hhigh[...], LANES - 1 - d, axis=1)
+    edge = pltpu.roll(hedge, LANES - 1 - 2 * d, axis=1)
     total = (
         fin[d, inner, :]
         + fin[d + 2, inner, :]
         + fin[d + 1, PAD - 1 : PAD + fin_rows - 1, :]
         + fin[d + 1, PAD + 1 : PAD + fin_rows + 1, :]
-        + lane_neighbours(here, low, high)
+        + lane_neighbours(here, edge, edge)
     )
     return here, total
 
@@ -218,7 +232,7 @@
         cells, rows, width = fluid_temp.shape
         depth, fin_rows, fin_width = fin_temp.shape
         assert rows == LANES and width == fin_width == 2 * rows and fin_rows == 2 * cells
-        assert depth <= LANES and depth % 8 == 0 and cells % 2 == 0 and rows % ROWS == 0 and fin_rows == ROWS
+        assert 2 * depth <= LANES and depth % 8 == 0 and cells % 2 == 0 and rows % ROWS == 0 and fin_rows == ROWS
         dims = (cells, rows, width, depth, fin_rows, fin_width)
         sizes = (groups, count)
         half = rows // 2
@@ -296,7 +310,7 @@
             (act, src, prev, nxt, below, above, side), refs = refs[2:9], refs[9:]
             wall_refs, refs = refs[: len(walls)], refs[len(walls) :]
             fluid, fin, first, rest, ghost_out, gxf, gxb, grpf, grpb, gyx = refs[:10]
-            zlow, zhigh, hlow, hhigh, deposit = refs[10:]
+            zrows, zedge, other, deposit = refs[10:]
             place = [lax.axis_index(name) for name in ("grp", "gx", "gy")]
             grp, gx, gy = place
             on_wall = grp == 0
@@ -338,12 +352,13 @@
                 deposit[...] = jnp.zeros((fin_rows, fin_width), jnp.float32)
 
             low_face = jnp.where(on_wall, ghost, below[0:cells, 0:LANES])
-            unpack_halos(fluid, fin, zlow, zhigh, hlow, hhigh, prev, nxt, below, above, side,
-                         low_face, place, sizes, dims)
-            fluid_sweep(fluid, act, zlow, zhigh, 0, dims)
+            unpack_halos(fluid, fin, zrows, zedge, prev, nxt, below, above, side, low_face, 0,
+                         place, sizes, dims)
+            fluid_sweep(fluid, act, zedge, other, 0, dims)
+            hedge = side[cells : cells + fin_rows, 0:LANES]
 
             def layer(d):
-                here, total = fin_neighbours(fin, d, hlow, hhigh, fin_rows)
+                here, total = fin_neighbours(fin, d, hedge, fin_rows)
                 rhs = here + src[d]
                 first[d + 1, PAD : PAD + fin_rows, :] = (rhs + FIN_CONDUCTION * total) * (1.0 / DIAG)
                 rest[d] = rhs * (OMEGA / DIAG) + here * (1.0 - OMEGA)
@@ -355,10 +370,9 @@
 
         received = (prev, nxt, below, above, side)
         scratch = [
+            pltpu.VMEM((LANES, rows), jnp.float32),
             pltpu.VMEM((rows, LANES), jnp.float32),
-            pltpu.VMEM((rows, LANES), jnp.float32),
-            pltpu.VMEM((fin_rows, LANES), jnp.float32),
-            pltpu.VMEM((fin_rows, LANES), jnp.float32),
+            pltpu.VMEM((rows + 2 * PAD, width), jnp.float32),
         ]
         outs = pl.pallas_call(
             middle_kernel,
@@ -381,28 +395,30 @@
 
         def end_kernel(_0, _1, _2, act, ghost, prev, nxt, below, above, side,
                        fluid, first, rest, fluid_new, fin_new,
-                       zlow, zhigh, hlow, hhigh, fluid_sems, fin_sems):
+                       zrows, zedge, other, fluid_sems, fin_sems):
             place = [lax.axis_index(name) for name in ("grp", "gx", "gy")]
             on_wall = place[0] == 0
             low_face = jnp.where(on_wall, ghost[...], below[0:cells, 0:LANES])
-            unpack_halos(fluid, first, zlow, zhigh, hlow, hhigh, prev, nxt, below, above, side,
-                         low_face, place, sizes, dims)
-
-            def fluid_copy(i):
+            unpack_halos(fluid, first, zrows, zedge, prev, nxt, below, above, side, low_face, 1,
+                         place, sizes, dims)
+            hedge = side[cells : cells + fin_rows, 0:LANES]
+
+            def fluid_copy(k):
                 return pltpu.make_async_copy(
-                    fluid.at[i + 1, pl.ds(PAD, rows), :], fluid_new.at[i], fluid_sems.at[i]
+                    fluid.at[pl.ds(2 * k + 1, 2), pl.ds(PAD, rows), :],
+                    fluid_new.at[pl.ds(2 * k, 2)], fluid_sems.at[k],
                 )
 
             def fin_copy(k):
                 part = pl.ds(k * 8, 8)
                 return pltpu.make_async_copy(rest.at[part], fin_new.at[part], fin_sems.at[k])
 
-            fluid_sweep(fluid, act, zlow, zhigh, 1, dims, lambda i: fluid_copy(i).start())
+            fluid_sweep(fluid, act, zedge, other, 1, dims, lambda k: fluid_copy(k).start())
 
             def layers(k, carry):
                 for j in range(8):
                     d = k * 8 + j
-                    _, total = fin_neighbours(first, d, hlow, hhigh, fin_rows)
+                    _, total = fin_neighbours(first, d, hedge, fin_rows)
                     rest[d] = rest[d] + (OMEGA * FIN_CONDUCTION / DIAG) * total
                 fin_copy(k).start()
                 return carry
@@ -417,7 +433,7 @@
                 fin_copy(d).wait()
                 return carry
 
-            lax.fori_loop(0, cells, finish_fluid, 0)
+            lax.fori_loop(0, cells // 2, finish_fluid, 0)
             lax.fori_loop(0, depth // 8, finish_fin, 0)
 
         results = pl.pallas_call(
@@ -426,7 +442,7 @@
                        f32(cells, rows, width), f32(depth, fin_rows, fin_width)),
             in_specs=[vmem] * 10,
             out_specs=(vmem, vmem, vmem, hbm, hbm),
-            scratch_shapes=scratch + [pltpu.SemaphoreType.DMA((cells,)),
+            scratch_shapes=scratch + [pltpu.SemaphoreType.DMA((cells // 2,)),
                                       pltpu.SemaphoreType.DMA((depth // 8,))],
             input_output_aliases={0: 0, 1: 1, 2: 2},
             compiler_params=params,

time: 42.6 us -> 39.9 us (0.937)
  Pallas kernels: 18.2 us -> 15.5 us
    pallas_call x1, Pallas kernels: 6.6 us -> 5.18 us  [local(): pl.pallas_call(end_kernel, out_shape=(fluid_pad, fin_pad, f32(depth, fin_...]
    pallas_call x1, Pallas kernels: 7.43 us -> 6.15 us  [local(): pl.pallas_call(middle_kernel, out_shape=(fluid_pad, fin_pad, fin_pad, f32...]
where the time goes in v4:
time: 39.9 us; the launch traced here: 39.8 us
  starting transfers between devices  16.5 us (41%)
  Pallas kernels  15.5 us (39%)
  waiting for transfers between devices  7.07 us (18%)
  between operations  0.7 us (2%)
    pallas_call x1, Pallas kernels, local(): pl.pallas_call(middle_kernel, out_shape=(fluid_pad, fin_pad, fin_pad, f32...  6.15 us
    ppermute x2, starting transfers between devices, local(): above = lax.ppermute(grpb, 'grp', around(groups, -1))  5.85 us
    pallas_call x1, Pallas kernels, local(): pl.pallas_call(end_kernel, out_shape=(fluid_pad, fin_pad, f32(depth, fin_...  5.18 us
    ppermute x2, waiting for transfers between devices, local(): below = lax.ppermute(grpf, 'grp', around(groups, 1))  4.6 us
    pallas_call x1, Pallas kernels, local(): pl.pallas_call(start_kernel, out_shape=(fluid_pad, fin_pad, f32(gx_rows,...  4.19 us
    ppermute x2, starting transfers between devices, local(): prev = lax.ppermute(gxf, 'gx', around(count, 1))  3.77 us
    ppermute x2, starting transfers between devices, local(): nxt = lax.ppermute(gxb, 'gx', around(count, -1))  3.25 us
    ppermute x1, waiting for transfers between devices, local(): lax.ppermute(wall, 'gx', around(count, k))  2.46 us
  transfers between devices with their start and end apart: 11, of which 3 were waited for; matrix products, arithmetic and copies ran while one was open for 0% of the time, Pallas kernels for 0%

profile of v4, /device:TPU:0, one launch (start us, length us, event | category | flops | bytes accessed | tf_op | source)
XLA Modules:
  0.0 39.8 jit_solution(10674185466752981725)
XLA Ops:
  0.6 0.0 copy-start
  0.6 0.0 copy-start.1
  0.7 4.2 %start.1 = (f32[18,144,256]{2,1,0:T(8,128)S(1)}, f32[66,48,256]{2,1,0:T(8,128)S(1)}, f32[176,256]{1,0:T(8,128)S(1)}, f32[176,256]{1,0:T(8,128)S(1)}, f32[48,256]...) custom-call(f32[16,128,256]{2,1,0:T(8,128)} %fluid_hbm.1, ...), custom_call_target="tpu_custom_call" | custom-call | tf_op jit(solution)/shard_map/start/pallas_call | solution.py:282
  4.9 3.0 %collective-permute-start = (f32[176,256]{1,0:T(8,128)S(1)}, f32[176,256]{1,0:T(8,128)S(1)}, u32[]{:S(2)}, u32[]{:S(2)}) collective-permute-start(f32[176,256]{1,0:T(8,128)S(1)} %get-tuple-element.23), channel_id=1, source_target_pairs={{0,2},{2,4},{4,6},{6,0},{1,3},{3,5},{5,7},{7,1},{8,10},{10,12},{12... | collective-permute-start | bytes 540680 | tf_op jit(solution)/shard_map/ppermute | solution.py:299
  7.9 1.0 %collective-permute-start.1 = (f32[176,256]{1,0:T(8,128)S(1)}, f32[176,256]{1,0:T(8,128)S(1)}, u32[]{:S(2)}, u32[]{:S(2)}) collective-permute-start(f32[176,256]{1,0:T(8,128)S(1)} %get-tuple-element.24), channel_id=1, source_target_pairs={{0,6},{2,0},{4,2},{6,4},{1,7},{3,1},{5,3},{7,5},{8,14},{10,8},{12,... | collective-permute-start | bytes 540680 | tf_op jit(solution)/shard_map/ppermute | solution.py:300
  8.9 2.0 %collective-permute-start.2 = (f32[48,256]{1,0:T(8,128)S(1)}, f32[48,256]{1,0:T(8,128)S(1)}, u32[]{:S(2)}, u32[]{:S(2)}) collective-permute-start(f32[48,256]{1,0:T(8,128)S(1)} %get-tuple-element.25), channel_id=1, source_target_pairs={{0,8},{8,16},{16,24},{24,0},{1,9},{9,17},{17,25},{25,1},{2,10},{10... | collective-permute-start | bytes 147464 | tf_op jit(solution)/shard_map/ppermute | solution.py:305
  10.9 2.0 %collective-permute-start.3 = (f32[48,256]{1,0:T(8,128)S(1)}, f32[48,256]{1,0:T(8,128)S(1)}, u32[]{:S(2)}, u32[]{:S(2)}) collective-permute-start(f32[48,256]{1,0:T(8,128)S(1)} %get-tuple-element.26), channel_id=1, source_target_pairs={{0,24},{8,0},{16,8},{24,16},{1,25},{9,1},{17,9},{25,17},{2,26},{10... | collective-permute-start | bytes 147464 | tf_op jit(solution)/shard_map/ppermute | solution.py:306
  12.9 0.0 collective-permute-start.4
  12.9 2.5 %collective-permute-done.2.refs_6_ = f32[48,256]{1,0:T(8,128)S(1)} collective-permute-done((f32[48,256]{1,0:T(8,128)S(1)}, f32[48,256]{1,0:T(8,128)S(1)}, u32[]{:S(2)}, u32[]{:S(2)}) %collective-permute-start.2) | collective-permute-done | bytes 49184 | tf_op jit(solution)/shard_map/ppermute | solution.py:305
  15.5 1.6 %collective-permute-start.5 = (f32[48,256]{1,0:T(8,128)S(1)}, f32[48,256]{1,0:T(8,128)S(1)}, u32[]{:S(2)}, u32[]{:S(2)}) collective-permute-start(f32[48,256]{1,0:T(8,128)S(1)} %get-tuple-element.28.refs_9_), channel_id=1, source_target_pairs={{0,4},{2,6},{4,0},{6,2},{1,5},{3,7},{5,1},{7,3},{8,12},{10,14},{12... | collective-permute-start | bytes 147464 | tf_op jit(solution)/shard_map/ppermute | solution.py:302
  17.1 0.0 collective-permute-done.3.refs_7_
  17.1 0.0 collective-permute-done.4.refs_8_
  17.1 2.5 %collective-permute-done.5.refs_10_ = f32[48,256]{1,0:T(8,128)S(1)} collective-permute-done((f32[48,256]{1,0:T(8,128)S(1)}, f32[48,256]{1,0:T(8,128)S(1)}, u32[]{:S(2)}, u32[]{:S(2)}) %collective-permute-start.5) | collective-permute-done | bytes 49184 | tf_op jit(solution)/shard_map/ppermute | solution.py:302
  19.5 0.0 collective-permute-done.refs_4_
  19.5 0.0 collective-permute-done.1.refs_5_
  19.5 0.0 copy-done
  19.6 0.0 copy-done.1
  19.6 6.2 %middle.1 = (f32[18,144,256]{2,1,0:T(8,128)S(1)}, f32[66,48,256]{2,1,0:T(8,128)S(1)}, f32[66,48,256]{2,1,0:T(8,128)S(1)}, f32[64,32,256]{2,1,0:T(8,128)S(1)}, f3...) custom-call(f32[18,144,256]{2,1,0:T(8,128)S(1)} %get-tuple-element.2, ...), custom_call_target="tpu_custom_call", output_to_operand_aliasing={{0}: (0, {}), {1}: (1, {})} | custom-call | tf_op jit(solution)/shard_map/middle/pallas_call | solution.py:377
  25.7 0.8 %collective-permute-start.6 = (f32[128,256]{1,0:T(8,128)S(1)}, f32[128,256]{1,0:T(8,128)S(1)}, u32[]{:S(2)}, u32[]{:S(2)}) collective-permute-start(f32[128,256]{1,0:T(8,128)S(1)} %get-tuple-element.33), channel_id=1, source_target_pairs={{0,2},{2,4},{4,6},{6,0},{1,3},{3,5},{5,7},{7,1},{8,10},{10,12},{12... | collective-permute-start | bytes 393224 | tf_op jit(solution)/shard_map/ppermute | solution.py:390
  26.5 2.2 %collective-permute-start.7 = (f32[128,256]{1,0:T(8,128)S(1)}, f32[128,256]{1,0:T(8,128)S(1)}, u32[]{:S(2)}, u32[]{:S(2)}) collective-permute-start(f32[128,256]{1,0:T(8,128)S(1)} %get-tuple-element.34), channel_id=1, source_target_pairs={{0,6},{2,0},{4,2},{6,4},{1,7},{3,1},{5,3},{7,5},{8,14},{10,8},{12,... | collective-permute-start | bytes 393224 | tf_op jit(solution)/shard_map/ppermute | solution.py:391
  28.7 0.0 collective-permute-start.8
  28.7 3.8 %collective-permute-start.9 = (f32[48,256]{1,0:T(8,128)S(1)}, f32[48,256]{1,0:T(8,128)S(1)}, u32[]{:S(2)}, u32[]{:S(2)}) collective-permute-start(f32[48,256]{1,0:T(8,128)S(1)} %get-tuple-element.36), channel_id=1, source_target_pairs={{0,24},{8,0},{16,8},{24,16},{1,25},{9,1},{17,9},{25,17},{2,26},{10... | collective-permute-start | bytes 147464 | tf_op jit(solution)/shard_map/ppermute | solution.py:393
  32.5 0.0 collective-permute-start.10
  32.5 2.1 %collective-permute-done.8.below = f32[48,256]{1,0:T(8,128)S(1)} collective-permute-done((f32[48,256]{1,0:T(8,128)S(1)}, f32[48,256]{1,0:T(8,128)S(1)}, u32[]{:S(2)}, u32[]{:S(2)}) %collective-permute-start.8) | collective-permute-done | bytes 49184 | tf_op jit(solution)/shard_map/ppermute | solution.py:392
  34.6 0.0 collective-permute-done.9.above
  34.6 0.0 collective-permute-done.10.side
  34.6 0.0 collective-permute-done.6.prev
  34.6 0.0 collective-permute-done.7.nxt
  34.6 5.2 %end.1 = (f32[18,144,256]{2,1,0:T(8,128)S(1)}, f32[66,48,256]{2,1,0:T(8,128)S(1)}, f32[64,32,256]{2,1,0:T(8,128)S(1)}, f32[16,128,256]{2,1,0:T(8,128)}, f32[64,32,256]{2,1,0:T(8,128)}) custom-call(f32[18,144,256]{2,1,0:T(8,128)S(1)} %get-tuple-element.29._0, ...), custom_call_target="tpu_custom_call", output_to_operand_aliasing={{0}: (0, {}), {1}: (1, {}), {2}: (2, {})} | custom-call | tf_op jit(solution)/shard_map/end/pallas_call | solution.py:439
Async XLA Ops:
  0.6 18.9 %copy-start = (s32[16,128,256]{2,1,0:T(8,128)S(1)}, s32[16,128,256]{2,1,0:T(8,128)}, u32[]{:S(2)}) copy-start(s32[16,128,256]{2,1,0:T(8,128)} %act.1) | copy-start | bytes 6291460
  0.6 18.9 %copy-start.1 = (f32[64,32,256]{2,1,0:T(8,128)S(1)}, f32[64,32,256]{2,1,0:T(8,128)}, u32[]{:S(2)}) copy-start(f32[64,32,256]{2,1,0:T(8,128)} %refs_3_.1) | copy-start | bytes 6291460
  4.9 14.7 %collective-permute-start = (f32[176,256]{1,0:T(8,128)S(1)}, f32[176,256]{1,0:T(8,128)S(1)}, u32[]{:S(2)}, u32[]{:S(2)}) collective-permute-start(f32[176,256]{1,0:T(8,128)S(1)} %get-tuple-element.23), channel_id=1, source_target_pairs={{0,2},{2,4},{4,6},{6,0},{1,3},{3,5},{5,7},{7,1},{8,10},{10,12},{12... | collective-permute-start | bytes 540680 | tf_op jit(solution)/shard_map/ppermute | solution.py:299
  7.9 11.7 %collective-permute-start.1 = (f32[176,256]{1,0:T(8,128)S(1)}, f32[176,256]{1,0:T(8,128)S(1)}, u32[]{:S(2)}, u32[]{:S(2)}) collective-permute-start(f32[176,256]{1,0:T(8,128)S(1)} %get-tuple-element.24), channel_id=1, source_target_pairs={{0,6},{2,0},{4,2},{6,4},{1,7},{3,1},{5,3},{7,5},{8,14},{10,8},{12,... | collective-permute-start | bytes 540680 | tf_op jit(solution)/shard_map/ppermute | solution.py:300
  8.9 6.6 %collective-permute-start.2 = (f32[48,256]{1,0:T(8,128)S(1)}, f32[48,256]{1,0:T(8,128)S(1)}, u32[]{:S(2)}, u32[]{:S(2)}) collective-permute-start(f32[48,256]{1,0:T(8,128)S(1)} %get-tuple-element.25), channel_id=1, source_target_pairs={{0,8},{8,16},{16,24},{24,0},{1,9},{9,17},{17,25},{25,1},{2,10},{10... | collective-permute-start | bytes 147464 | tf_op jit(solution)/shard_map/ppermute | solution.py:305
  10.9 6.2 %collective-permute-start.3 = (f32[48,256]{1,0:T(8,128)S(1)}, f32[48,256]{1,0:T(8,128)S(1)}, u32[]{:S(2)}, u32[]{:S(2)}) collective-permute-start(f32[48,256]{1,0:T(8,128)S(1)} %get-tuple-element.26), channel_id=1, source_target_pairs={{0,24},{8,0},{16,8},{24,16},{1,25},{9,1},{17,9},{25,17},{2,26},{10... | collective-permute-start | bytes 147464 | tf_op jit(solution)/shard_map/ppermute | solution.py:306
  12.9 4.2 %collective-permute-start.4 = (f32[48,256]{1,0:T(8,128)S(1)}, f32[48,256]{1,0:T(8,128)S(1)}, u32[]{:S(2)}, u32[]{:S(2)}) collective-permute-start(f32[48,256]{1,0:T(8,128)S(1)} %get-tuple-element.27), channel_id=1, source_target_pairs={{0,1},{1,0},{2,3},{3,2},{4,5},{5,4},{6,7},{7,6},{8,9},{9,8},{10,11... | collective-permute-start | bytes 147464 | tf_op jit(solution)/shard_map/ppermute | solution.py:307
  15.5 4.1 %collective-permute-start.5 = (f32[48,256]{1,0:T(8,128)S(1)}, f32[48,256]{1,0:T(8,128)S(1)}, u32[]{:S(2)}, u32[]{:S(2)}) collective-permute-start(f32[48,256]{1,0:T(8,128)S(1)} %get-tuple-element.28.refs_9_), channel_id=1, source_target_pairs={{0,4},{2,6},{4,0},{6,2},{1,5},{3,7},{5,1},{7,3},{8,12},{10,14},{12... | collective-permute-start | bytes 147464 | tf_op jit(solution)/shard_map/ppermute | solution.py:302
  25.7 8.9 %collective-permute-start.6 = (f32[128,256]{1,0:T(8,128)S(1)}, f32[128,256]{1,0:T(8,128)S(1)}, u32[]{:S(2)}, u32[]{:S(2)}) collective-permute-start(f32[128,256]{1,0:T(8,128)S(1)} %get-tuple-element.33), channel_id=1, source_target_pairs={{0,2},{2,4},{4,6},{6,0},{1,3},{3,5},{5,7},{7,1},{8,10},{10,12},{12... | collective-permute-start | bytes 393224 | tf_op jit(solution)/shard_map/ppermute | solution.py:390
  26.5 8.1 %collective-permute-start.7 = (f32[128,256]{1,0:T(8,128)S(1)}, f32[128,256]{1,0:T(8,128)S(1)}, u32[]{:S(2)}, u32[]{:S(2)}) collective-permute-start(f32[128,256]{1,0:T(8,128)S(1)} %get-tuple-element.34), channel_id=1, source_target_pairs={{0,6},{2,0},{4,2},{6,4},{1,7},{3,1},{5,3},{7,5},{8,14},{10,8},{12,... | collective-permute-start | bytes 393224 | tf_op jit(solution)/shard_map/ppermute | solution.py:391
  28.7 5.9 %collective-permute-start.8 = (f32[48,256]{1,0:T(8,128)S(1)}, f32[48,256]{1,0:T(8,128)S(1)}, u32[]{:S(2)}, u32[]{:S(2)}) collective-permute-start(f32[48,256]{1,0:T(8,128)S(1)} %get-tuple-element.35), channel_id=1, source_target_pairs={{0,8},{8,16},{16,24},{24,0},{1,9},{9,17},{17,25},{25,1},{2,10},{10... | collective-permute-start | bytes 147464 | tf_op jit(solution)/shard_map/ppermute | solution.py:392
  28.7 5.9 %collective-permute-start.9 = (f32[48,256]{1,0:T(8,128)S(1)}, f32[48,256]{1,0:T(8,128)S(1)}, u32[]{:S(2)}, u32[]{:S(2)}) collective-permute-start(f32[48,256]{1,0:T(8,128)S(1)} %get-tuple-element.36), channel_id=1, source_target_pairs={{0,24},{8,0},{16,8},{24,16},{1,25},{9,1},{17,9},{25,17},{2,26},{10... | collective-permute-start | bytes 147464 | tf_op jit(solution)/shard_map/ppermute | solution.py:393
  32.5 2.1 %collective-permute-start.10 = (f32[48,256]{1,0:T(8,128)S(1)}, f32[48,256]{1,0:T(8,128)S(1)}, u32[]{:S(2)}, u32[]{:S(2)}) collective-permute-start(f32[48,256]{1,0:T(8,128)S(1)} %get-tuple-element.37), channel_id=1, source_target_pairs={{0,1},{1,0},{2,3},{3,2},{4,5},{5,4},{6,7},{7,6},{8,9},{9,8},{10,11... | collective-permute-start | bytes 147464 | tf_op jit(solution)/shard_map/ppermute | solution.py:394
